TPU v7x, 512 devices: a whole 4x8x8 slice. The times are simulated.
512 devices in a mesh: sys: 32 (over y_hi, z, core), graph: 16 (over y_lo, x).
Axes of the slice: x: 4, y: 8 (y_hi: 2, y_lo: 4; y = y_hi * 4 + y_lo), z: 8, core: 2. Of those that a mesh axis runs over, the one named last changes fastest.
Arguments:
- node_features: bfloat16 [32, 256, 25, 128], P('sys', 'graph'), may hold values from -6 to 6
- atom_slot: int32 [32, 256], P('sys'), may hold values from 0 to 255, each once within a row
- neighbour: int32 [32, 18432], P('sys', 'graph'), may hold values from 0 to 255
- pad_mask: int32 [32, 18432], P('sys', 'graph'), may hold values 0 or 1
- envelope: float32 [32, 18432], P('sys', 'graph'), may hold values from 0.1 to 1
- wigner_rows: bfloat16 [32, 13, 25, 18432], P('sys', None, None, 'graph'), may hold values from -1.1953125 to 1.1953125
- mix_table: float32 [32, 32], replicated, may hold values from 0.1 to 2
- zero_weight: bfloat16 [32, 640, 640], P('sys', 'graph'), may hold values from -0.0390625 to 0.0390625
- one_weight: bfloat16 [32, 512, 2, 512], P('sys', 'graph'), may hold values from -0.03125 to 0.03125
Outputs:
- update: bfloat16 [32, 256, 25, 128], P('sys', 'graph')
Inputs may be any that keep to these rules, and one draw needn't show every extreme that they name: `neighbour`: atom ids of the edge's own system; edge slots a * 72 to a * 72 + 71 belong to the atom in row a of node_features. `atom_slot`: each system's row names every row of node_features once.
All inputs are finite; a program needn't handle non-finite values. No bound on the sum of `pad_mask` on one device may be relied on, other than what follows from the above.
Results may differ from a plain program's by a relative error of at most 0.025.
Values may be sent and summed in bfloat16 or wider, within the bound.
No kernel may reach another device: no remote copies, remote signals or barrier semaphores. Data moves between devices by JAX's collectives and lax.ppermute only.
A program may use at most 64 MiB of HBM per device.

v0:
```python
import math

import jax
import jax.numpy as jnp
from jax import lax
from jax.sharding import Mesh
from jax.sharding import PartitionSpec as P

LMAX = 4
NEIGH = 72
GRAPH = ("graph_0", "graph_1")


def in_one_piece(arrays, axis, dim, along):
    widths = [math.prod(a.shape[along:]) for a in arrays]
    both = jnp.concatenate(
        [a.reshape(*a.shape[:along], w) for a, w in zip(arrays, widths)], axis=along
    )
    whole = lax.all_gather(both, axis, axis=dim, tiled=True)
    pieces = jnp.split(whole, [sum(widths[:k]) for k in range(1, len(widths))], axis=along)
    return tuple(
        (b.reshape(*whole.shape[:along], *a.shape[along:]) for a, b in zip(arrays, pieces))
    )


def joined_along(pieces, dim):
    pieces = jnp.moveaxis(pieces, 0, dim)
    shape = pieces.shape
    return pieces.reshape(*shape[:dim], shape[dim] * shape[dim + 1], *shape[dim + 2 :])


def all_blocks(shard, axes, order):
    pieces = shard[None]
    for k in order:
        pieces = lax.all_gather(pieces, axes[k], axis=0, tiled=True)
    current = [lax.axis_size(axes[k]) for k in reversed(order)]
    pieces = pieces.reshape(*current, *shard.shape)
    turned = sorted(range(len(order)), key=lambda place: order[len(order) - 1 - place])
    return pieces.transpose(*turned, *range(len(order), pieces.ndim)).reshape(-1, *shard.shape)


def gathered_by_axis(shard, axes, order, dim):
    return joined_along(all_blocks(shard, axes, order), dim)


def copy_for_each(shard, axis):
    peers = lax.axis_size(axis)
    return lax.all_to_all(
        jnp.broadcast_to(shard[None], (peers, *shard.shape)), axis, 0, 0, tiled=True
    )


def collect(shard, axis, dim):
    return joined_along(copy_for_each(shard, axis), dim)


def scaled_term(factor, weight):
    term = (factor * weight.astype(jnp.float32)).astype(jnp.bfloat16)
    term = lax.optimization_barrier(term)
    return term.astype(jnp.float32)


def shards(
    node_features,
    atom_slot,
    neighbour,
    pad_mask,
    envelope,
    wigner_rows,
    mix_table,
    zero_weight,
    one_weight,
):
    sys_index = lax.axis_index("sys")
    every_zero, every_one = in_one_piece((zero_weight, one_weight), "sys", 0, 1)
    factors = lax.dynamic_slice_in_dim(mix_table, sys_index, 1, 0)[0]
    merged_zero = jnp.sum(scaled_term(factors[:, None, None], every_zero), axis=0)
    merged_one = jnp.sum(scaled_term(factors[:, None, None, None], every_one), axis=0)
    merged_zero = merged_zero.astype(jnp.bfloat16)
    merged_one = merged_one.astype(jnp.bfloat16)
    features = gathered_by_axis(node_features, GRAPH, (0, 1), 1)[0]
    source_rows = jnp.take(atom_slot[0], neighbour[0], axis=0)
    sources = jnp.take(features, source_rows, axis=0)
    frame_local = wigner_rows[0]
    rotated = jnp.einsum(
        "rke,ekc->erc", frame_local, sources, preferred_element_type=jnp.float32
    ).astype(jnp.bfloat16)
    edge_count = rotated.shape[0]
    channels = rotated.shape[2]
    first = rotated[:, : LMAX + 1].reshape(edge_count, -1)
    others = rotated[:, LMAX + 1 :].reshape(edge_count, -1)
    edge_gate = envelope[0] * pad_mask[0].astype(jnp.float32)
    result = lax.dot_general(
        first,
        collect(merged_zero, GRAPH, 0),
        (((1,), (1,)), ((), ())),
        preferred_element_type=jnp.float32,
    )
    out_zero = (edge_gate[:, None] * result).astype(jnp.bfloat16)
    segment = collect(merged_one, GRAPH, 0)
    real_part = segment[:, 0]
    imag_part = segment[:, 1]
    piece_count = segment.shape[0]
    stacked = jnp.stack(
        [
            jnp.concatenate([real_part, -imag_part], axis=1),
            jnp.concatenate([imag_part, real_part], axis=1),
        ],
        axis=0,
    )
    result = lax.dot_general(
        others,
        stacked.reshape(2 * piece_count, -1),
        (((1,), (1,)), ((), ())),
        preferred_element_type=jnp.float32,
    )
    out_one = (edge_gate[:, None] * result).astype(jnp.bfloat16).reshape(edge_count, 2, piece_count)
    atom_count = edge_count // NEIGH
    harmonics = frame_local.shape[1]
    near_part = jnp.einsum(
        "rkaj,ajrc->akc",
        frame_local[: LMAX + 1].reshape(LMAX + 1, harmonics, atom_count, NEIGH),
        out_zero.reshape(atom_count, NEIGH, LMAX + 1, channels),
        preferred_element_type=jnp.float32,
    )
    far_part = jnp.einsum(
        "rkaj,ajrc->akc",
        frame_local[LMAX + 1 :].reshape(2 * LMAX, harmonics, atom_count, NEIGH),
        out_one.reshape(atom_count, NEIGH, 2 * LMAX, channels),
        preferred_element_type=jnp.float32,
    )
    update = ((near_part + far_part) * (1.0 / math.sqrt(NEIGH))).astype(jnp.bfloat16)
    return update[None]


def solution(mesh):
    finer = Mesh(mesh.devices.reshape(mesh.shape["sys"], 4, 4), ("sys", "graph_0", "graph_1"))
    return jax.shard_map(
        shards,
        mesh=finer,
        in_specs=(
            P("sys", GRAPH, None, None),
            P("sys", None),
            P("sys", GRAPH),
            P("sys", GRAPH),
            P("sys", GRAPH),
            P("sys", None, None, GRAPH),
            P(),
            P("sys", GRAPH, None),
            P("sys", GRAPH, None, None),
        ),
        out_specs=P("sys", GRAPH, None, None),
        check_vma=False,
    )
```

profile of v0, /device:TPU:6, one launch (start us, length us, event | category | flops | bytes accessed | tf_op | source)
XLA Modules:
  0.0 230.6 jit_solution(10309182245357668896)
XLA Ops:
  6.5 0.0 all-gather.8.cloned.1.call-start
  6.5 1.0 reshape.138
  7.5 0.9 copy.61
  8.4 0.9 maximum_bitcast_fusion.2
  9.4 0.0 all-gather.8.cloned.1.call-update
  9.4 0.0 all-gather.6.cloned.1.call-start
  9.4 16.8 %all-gather = bf16[4,16,25,128]{3,1,2,0:T(8,128)(2,1)} all-gather(bf16[1,16,25,128]{3,1,2,0:T(8,128)(2,1)} %param.9), channel_id=2, replica_groups=mesh['sys'=32,'graph_0'=4,'graph_1'=4] {'graph_0'}, dimensions={0}, use_global_device_ids=true | all-gather | bytes 512000 | tf_op jit(solution)/shard_map/all_gather | solution.py:35
  26.2 0.0 all-gather.6.cloned.1.call-update
  26.2 1.1 slice.21
  27.3 0.1 slice.25
  27.4 0.0 copy-start.9
  27.4 0.0 copy-start.2
  27.5 5.0 %copy.46 = bf16[13,25,1152]{1,0,2:T(8,128)(2,1)} copy(bf16[13,25,1152]{2,0,1:T(8,128)(2,1)S(1)} %bitcast.101) | data formatting | bytes 1497600 | tf_op jit(solution)/shard_map/squeeze | solution.py:84
  32.5 0.0 copy-done.2
  32.5 7.3 %gather_fusion = s32[1152]{0:T(1024)S(1)} fusion(s32[256]{0:T(256)S(1)} %bitcast.92, s32[2048]{0:T(1024)S(1)} %pad_clamp_fusion.1), kind=kCustom, calls=%fused_computation | custom fusion | bytes 13824 | tf_op jit(solution)/shard_map/jit(_take)/gather | solution.py:82
  39.8 1.8 reshape.171
  41.6 2.8 %copy.59 = bf16[1,8,25,1152]{2,1,3,0:T(8,128)(2,1)} copy(bf16[1,8,25,1152]{3,1,2,0:T(8,128)(2,1)S(1)} %slice.25) | data formatting | bytes 921600 | tf_op jit(solution)/shard_map/reshape | solution.py:128
  44.4 0.0 copy-done
  44.4 99.1 %all-gather.8.cloned.1.call-done = bf16[32,1,58368]{2,1,0:T(2,128)(2,1)} async-done(((bf16[1,1,58368]{2,1,0:T(2,128)(2,1)}), bf16[32,1,58368]{2,1,0:T(2,128)(2,1)}) %all-gather.8.cloned.1.call-update) | async-done | bytes 3735568 | tf_op jit(solution)/shard_map/all_gather | solution.py:19
  143.6 4.3 %copy.78 = bf16[32,1,58368]{2,0,1:T(8,128)(2,1)S(1)} copy(bf16[32,1,58368]{2,1,0:T(2,128)(2,1)} %all-gather.8.cloned.1.call-done) | data formatting | bytes 7471104
  147.9 0.2 slice_convert_fusion.1
  148.1 1.6 copy-done.3
  149.7 0.6 copy.62
  150.3 0.3 fusion.5
  150.6 0.2 reduce_sum.24
  150.9 1.0 broadcast_in_dim.43
  151.9 5.2 %all-to-all-start = ((bf16[16,40,640]{2,1,0:T(8,128)(2,1)}), bf16[16,40,640]{2,1,0:T(8,128)(2,1)S(1)}, u32[]{:S(2)}, u32[]{:S(2)}) async-start(bf16[16,40,640]{2,1,0:T(8,128)(2,1)} %broadcast_in_dim.43), calls=%async_computation | async-start | bytes 1638400 | tf_op jit(solution)/shard_map/all_to_all | solution.py:48
  157.1 3.8 %slice_convert_fusion = f32[32,32768]{1,0:T(8,128)} fusion(bf16[32,58368]{1,0:T(8,128)(2,1)} %bitcast.94), kind=kLoop, calls=%fused_computation.19 | loop fusion | flops 1048576 | bytes 6291456 | tf_op jit(solution)/shard_map/convert_element_type | solution.py:58
  160.9 6.6 %reshape.147 = f32[32,32,2,512]{3,2,1,0:T(2,128)} reshape(f32[32,32768]{1,0:T(8,128)} %slice_convert_fusion) | data formatting | bytes 8388608 | tf_op jit(solution)/shard_map/convert_element_type | solution.py:58
  167.5 4.2 %multiply_convert_fusion = bf16[32,32,2,512]{3,2,1,0:T(2,128)(2,1)S(1)} fusion(f32[32,32,2,512]{3,2,1,0:T(2,128)} %reshape.147, f32[32]{0:T(128)S(1)} %dynamic-slice_bitcast_fusion), kind=kLoop, calls=%fused_computation.8 | loop fusion | flops 2097152 | bytes 6291584 | tf_op jit(solution)/shard_map/convert_element_type | solution.py:58
  171.7 0.0 copy-start.10
  171.8 0.0 copy-start.11
  171.8 2.0 reduce_sum.25
  173.8 3.1 %all-to-all-done = bf16[16,40,640]{2,1,0:T(8,128)(2,1)S(1)} async-done(((bf16[16,40,640]{2,1,0:T(8,128)(2,1)}), bf16[16,40,640]{2,1,0:T(8,128)(2,1)S(1)}, u32[]{:S(2)}, u32[]{:S(2)}) %all-to-all-start) | async-done | bytes 819232 | tf_op jit(solution)/shard_map/all_to_all | solution.py:48
  176.9 1.2 broadcast_in_dim.44
  178.1 0.0 copy-done.7
  178.1 6.8 %all-to-all-start.1 = ((bf16[16,32,2,512]{3,1,2,0:T(8,128)(2,1)}), bf16[16,32,2,512]{3,1,2,0:T(8,128)(2,1)S(1)}, u32[]{:S(2)}, u32[]{:S(2)}) async-start(bf16[16,32,2,512]{3,1,2,0:T(8,128)(2,1)} %broadcast_in_dim.44), calls=%async_computation.1 | async-start | bytes 2097152 | tf_op jit(solution)/shard_map/all_to_all | solution.py:48
  184.9 0.0 all-gather.6.cloned.1.call-done
  185.0 1.9 copy.44
  186.9 1.1 copy.45
  188.0 6.1 %gather_fusion.1 = bf16[1152,25,128]{2,1,0:T(8,128)(2,1)} fusion(bf16[256,25,128]{2,1,0:T(8,128)(2,1)S(1)} %copy.45, s32[2048]{0:T(1024)S(1)} %pad_clamp_fusion), kind=kCustom, calls=%fused_computation.1 | custom fusion | bytes 14750208 | tf_op jit(solution)/shard_map/jit(_take)/gather | solution.py:83
  194.1 7.2 %convert_bitcast_fusion = bf16[1152,13,128]{2,1,0:T(8,128)(2,1)S(1)} fusion(bf16[13,25,1152]{1,0,2:T(8,128)(2,1)} %copy.46, bf16[1152,25,128]{2,1,0:T(8,128)(2,1)} %gather_fusion.1, pred[1152]{0:T(1024)(128)(4,1)S(1)} %compare_and_fusion), kind=kOutput, calls=%fused_computation.6 | convolution fusion | flops 101449728 | bytes 11956608 | tf_op jit(solution)/shard_map/rke,ekc->erc/dot_general | solution.py:85
  201.3 0.2 slice.30
  201.5 1.8 slice.31
  203.3 2.4 %copy.47 = bf16[1152,5,128]{0,2,1:T(8,128)(2,1)} copy(bf16[1152,5,128]{2,1,0:T(8,128)(2,1)S(1)} %slice.30) | data formatting | bytes 2949120 | tf_op jit(solution)/shard_map/slice | solution.py:90
  205.7 4.2 %fusion.6 = bf16[1152,640]{1,0:T(8,128)(2,1)} fusion(bf16[1152,640]{0,1:T(8,128)(2,1)} %bitcast.105, bf16[640,640]{1,0:T(8,128)(2,1)} %bitcast.106, f32[1152]{0:T(1024)S(1)} %multiply_reduce_fusion), kind=kOutput, calls=%fused_computation.14 | convolution fusion | flops 945192960 | bytes 3772928 | tf_op jit(solution)/shard_map/dot_general | solution.py:93
  210.0 3.3 %reshape.140 = bf16[16,72,5,128]{3,2,1,0:T(8,128)(2,1)S(1)} reshape(bf16[1152,640]{1,0:T(8,128)(2,1)} %fusion.6) | data formatting | bytes 2949120 | tf_op jit(solution)/shard_map/reshape | solution.py:123
  213.2 2.2 fusion.21
  215.5 0.0 all-to-all-done.1
  215.5 0.1 copy.52
  215.6 0.1 slice_bitcast_fusion
  215.7 0.3 maximum_bitcast_fusion
  216.0 0.0 copy-start.6
  216.0 0.2 pad_maximum_fusion
  216.2 1.5 copy-done.6
  217.7 2.9 %fusion.13 = bf16[144,8,8,128]{3,1,2,0:T(8,128)(2,1)S(1)} fusion(bf16[1024,1024]{1,0:T(8,128)(2,1)S(1)} %bitcast.103, bf16[144,8,8,128]{3,2,1,0:T(8,128)(2,1)S(1)} %bitcast.102, f32[1152]{0:T(1024)S(1)} %multiply_reduce_fusion), kind=kOutput, calls=%fused_computation.21 | convolution fusion | flops 2418278400 | bytes 6820352 | tf_op jit(solution)/shard_map/dot_general | solution.py:111
  220.6 0.0 copy-start.4
  220.6 0.0 copy-start.8
  220.6 0.7 copy.64
  221.3 0.0 copy-start.1
  221.3 1.0 copy-done.4
  222.2 0.0 copy-done.8
  222.3 0.8 fusion.33
  223.1 0.7 copy.54
  (19 shorter events, 0.2 us)
Async XLA Ops:
  6.5 37.9 %copy-start = (f32[32,32]{1,0:T(8,128)S(1)}, f32[32,32]{1,0:T(8,128)}, u32[]{:S(2)}) copy-start(f32[32,32]{1,0:T(8,128)} %param.15) | copy-start | bytes 12292
  6.5 20.7 %copy-start.5 = (bf16[1,13,25,1152]{3,1,2,0:T(8,128)(2,1)S(1)}, bf16[1,13,25,1152]{3,1,2,0:T(8,128)(2,1)}, u32[]{:S(2)}) copy-start(bf16[1,13,25,1152]{3,1,2,0:T(8,128)(2,1)} %param.14) | copy-start | bytes 2246404
  6.5 137.0 %all-gather.8.cloned.1.call-start = ((), (), s32[]{:S(2)}) async-start(), calls=%async_computation.3 | async-start | bytes 7704576 | tf_op jit(solution)/shard_map/all_gather | solution.py:19
  9.4 175.6 %all-gather.6.cloned.1.call-start = ((), (), s32[]{:S(2)}) async-start(), calls=%async_computation.2 | async-start | bytes 2048000 | tf_op jit(solution)/shard_map/all_gather | solution.py:35
  27.4 5.0 %copy-start.9 = (s32[1,1152]{1,0:T(1,128)S(1)}, s32[1,1152]{1,0:T(1,128)}, u32[]{:S(2)}) copy-start(s32[1,1152]{1,0:T(1,128)} %param.11) | copy-start | bytes 13828
  27.4 5.0 %copy-start.2 = (s32[1,256]{1,0:T(1,128)S(1)}, s32[1,256]{1,0:T(1,128)}, u32[]{:S(2)}) copy-start(s32[1,256]{1,0:T(1,128)} %param.10) | copy-start | bytes 3076
  147.9 1.8 copy-start.3
  151.9 25.0 %all-to-all-start = ((bf16[16,40,640]{2,1,0:T(8,128)(2,1)}), bf16[16,40,640]{2,1,0:T(8,128)(2,1)S(1)}, u32[]{:S(2)}, u32[]{:S(2)}) async-start(bf16[16,40,640]{2,1,0:T(8,128)(2,1)} %broadcast_in_dim.43), calls=%async_computation | async-start | bytes 1638400 | tf_op jit(solution)/shard_map/all_to_all | solution.py:48
  171.7 13.1 %copy-start.10 = (f32[1,1152]{1,0:T(1,128)S(1)}, f32[1,1152]{1,0:T(1,128)}, u32[]{:S(2)}) copy-start(f32[1,1152]{1,0:T(1,128)} %param.13) | copy-start | bytes 13828
  171.8 13.1 %copy-start.11 = (s32[1,1152]{1,0:T(1,128)S(1)}, s32[1,1152]{1,0:T(1,128)}, u32[]{:S(2)}) copy-start(s32[1,1152]{1,0:T(1,128)} %param.12) | copy-start | bytes 13828
  176.9 1.2 copy-start.7
  178.1 37.4 %all-to-all-start.1 = ((bf16[16,32,2,512]{3,1,2,0:T(8,128)(2,1)}), bf16[16,32,2,512]{3,1,2,0:T(8,128)(2,1)S(1)}, u32[]{:S(2)}, u32[]{:S(2)}) async-start(bf16[16,32,2,512]{3,1,2,0:T(8,128)(2,1)} %broadcast_in_dim.44), calls=%async_computation.1 | async-start | bytes 2097152 | tf_op jit(solution)/shard_map/all_to_all | solution.py:48
  216.0 1.7 copy-start.6
  220.6 1.7 copy-start.4
  220.6 1.7 copy-start.8
  221.3 2.5 %copy-start.1 = (f32[32,32]{1,0:T(8,128)S(1)}, f32[32,32]{1,0:T(8,128)}, u32[]{:S(2)}) copy-start(f32[32,32]{1,0:T(8,128)} %param.15) | copy-start | bytes 12292
Sparse Core Ops, SparseCore 0:
  10.6 132.9 all-gather.7
  145.7 32.8 all-gather.5
where the time goes:
time: 232 us; the launch traced here: 231 us
  waiting for transfers between devices  102 us (44%)
  local copies, waits for them, and re-layouts  56.1 us (24%)
  matrix products  17.4 us (7%)
  blocking collectives  16.8 us (7%)
  between operations  13.7 us (6%)
  other arithmetic  12.4 us (5%)
  starting transfers between devices  12 us (5%)
    all_gather x1, waiting for transfers between devices, in_one_piece(): whole = lax.all_gather(both, axis, axis=dim, tiled=True)  99.1 us
    all_gather x1, blocking collectives, all_blocks(): pieces = lax.all_gather(pieces, axes[k], axis=0, tiled=True)  16.8 us
    all_to_all x2, starting transfers between devices, copy_for_each(): lax.all_to_all(jnp.broadcast_to(shard[None], (peers, *shard.shape)), axis...  12 us
    unnamed x28, local copies, waits for them, and re-layouts  10.6 us
    convert_element_type x4, other arithmetic, scaled_term(): term = (factor * weight.astype(jnp.float32)).astype(jnp.bfloat16)  8.54 us
    gather x1, local copies, waits for them, and re-layouts, shards(): source_rows = jnp.take(atom_slot[0], neighbour[0], axis=0)  7.25 us
    dot_general x1, matrix products, shards(): jnp.einsum('rke,ekc->erc', frame_local, sources, preferred_element_type=j...  7.21 us
    convert_element_type x1, local copies, waits for them, and re-layouts, scaled_term(): term = (factor * weight.astype(jnp.float32)).astype(jnp.bfloat16)  6.62 us
  transfers between devices with their start and end apart: 4, of which 2 were waited for; matrix products, arithmetic and copies ran while one was open for 32% of the time, Pallas kernels for 0%

commit v1 on v0

v1 whole, which is shorter than its diff:
```python
import math

import jax
import jax.numpy as jnp
from jax import lax
from jax.experimental import pallas as pl
from jax.experimental.pallas import tpu as pltpu
from jax.sharding import Mesh
from jax.sharding import PartitionSpec as P


LMAX = 4
NEIGH = 72
SYS = ("yh", "z", "c")
GRAPH = ("yl", "x")
LANES = 128
PAD = 32
GROUP = 8
MIB = 1024 * 1024


def turned(value, axis, by):
    size = lax.axis_size(axis)
    return lax.ppermute(value, axis, [(i, (i + by) % size) for i in range(size)])


def copies_from_all(value, axis):
    size = math.prod(lax.axis_size(a) for a in axis) if isinstance(axis, tuple) else lax.axis_size(axis)
    spread = jnp.broadcast_to(value[None], (size, *value.shape))
    return lax.all_to_all(spread, axis, 0, 0, tiled=True)


def lane_tiles(rows):
    height, width = rows.shape
    return rows.reshape(height // 8, 8, width // LANES, LANES).transpose(0, 2, 1, 3).reshape(-1, LANES)


def merge_kernel(factor_ref, chunk_ref, send_ref, other_ref, own_ref):
    zs, tiles = chunk_ref.shape[:2]
    targets = (
        (own_ref, [factor_ref[0, k] for k in range(zs)]),
        (send_ref.at[0], [factor_ref[1, k] for k in range(zs)]),
        (other_ref, [factor_ref[2, k] for k in range(zs)]),
        (send_ref.at[1], [factor_ref[3, k] for k in range(zs)]),
    )
    for j in range(tiles):
        pieces = [chunk_ref[k, j].astype(jnp.float32) for k in range(zs)]
        for ref, by in targets:
            total = by[0] * pieces[0]
            for k in range(1, zs):
                total = total + by[k] * pieces[k]
            ref[j] = total.astype(ref.dtype)


def partial_sums(factors, chunks):
    zs, rows, lanes = chunks.shape
    tiles = rows // 8
    one = jax.ShapeDtypeStruct((tiles, 8, lanes), jnp.bfloat16)
    vmem = pl.BlockSpec(memory_space=pltpu.VMEM)
    smem = pl.BlockSpec(memory_space=pltpu.SMEM)
    outs = pl.pallas_call(
        merge_kernel,
        out_shape=(jax.ShapeDtypeStruct((2, tiles, 8, lanes), jnp.bfloat16), one, one),
        in_specs=[smem, vmem],
        out_specs=(vmem, vmem, vmem),
        compiler_params=pltpu.CompilerParams(vmem_limit_bytes=12 * MIB),
        name="merge_experts",
    )(factors, chunks.reshape(zs, tiles, 8, lanes))
    return tuple(o.reshape(-1, rows, lanes) if o.ndim == 4 else o.reshape(rows, lanes) for o in outs)


def rotate_kernel(slot_ref, neighbour_ref, *refs):
    piece_refs = refs[:4]
    wigner_ref, out_ref, feature_ref, spread_ref = refs[4:]
    frame = wigner_ref.shape[0]
    atoms, harmonics = piece_refs[0].shape[:2]
    for k, ref in enumerate(piece_refs):
        feature_ref[k * atoms : (k + 1) * atoms, :harmonics] = ref[...]
    feature_ref[:, harmonics:] = jnp.zeros_like(feature_ref[:, harmonics:])
    width = GROUP * PAD
    block = LANES
    column = lax.broadcasted_iota(jnp.int32, (PAD, width), 1)
    row = lax.broadcasted_iota(jnp.int32, (PAD, width), 0)
    repeat = (column % PAD == row).astype(jnp.bfloat16)
    edge = lax.broadcasted_iota(jnp.int32, (block, width), 0)
    lane = lax.broadcasted_iota(jnp.int32, (block, width), 1)
    own = edge % GROUP == lane // PAD

    def one_block(b, carry):
        start = pl.multiple_of(b * block, block)
        for r in range(frame):
            part = lax.dot_general(
                wigner_ref[r, :, pl.ds(start, block)],
                repeat,
                (((0,), (0,)), ((), ())),
                preferred_element_type=jnp.float32,
            )
            spread_ref[r] = jnp.where(own, part, 0.0)
        for pair in range(block // (2 * GROUP)):
            halves = []
            for half in range(2):
                low = (2 * pair + half) * GROUP
                tiles = []
                for e in range(GROUP):
                    source = slot_ref[neighbour_ref[start + low + e]]
                    tiles.append(feature_ref[source])
                stacked = jnp.concatenate(tiles, axis=0)
                rows = jnp.concatenate(
                    [spread_ref[r, low : low + GROUP, :] for r in range(frame)], axis=0
                ).astype(jnp.bfloat16)
                halves.append(
                    lax.dot_general(
                        rows, stacked, (((1,), (0,)), ((), ())), preferred_element_type=jnp.float32
                    )
                )
            for r in range(frame):
                both = jnp.concatenate([h[GROUP * r : GROUP * (r + 1)] for h in halves], axis=0)
                out_ref[
                    pl.ds(pl.multiple_of(start + 2 * GROUP * pair, 2 * GROUP), 2 * GROUP),
                    r * LANES : (r + 1) * LANES,
                ] = both.astype(out_ref.dtype)
        return carry

    lax.fori_loop(0, neighbour_ref.shape[0] // block, one_block, 0)


def rotate(slots, neighbour, pieces, wigner):
    frame, _, edges = wigner.shape
    atoms = len(pieces) * pieces[0].shape[0]
    return pl.pallas_call(
        rotate_kernel,
        out_shape=jax.ShapeDtypeStruct((edges, frame * LANES), jnp.bfloat16),
        in_specs=[
            pl.BlockSpec(memory_space=pltpu.SMEM),
            pl.BlockSpec(memory_space=pltpu.SMEM),
        ]
        + [pl.BlockSpec(memory_space=pltpu.VMEM)] * (len(pieces) + 1),
        out_specs=pl.BlockSpec(memory_space=pltpu.VMEM),
        scratch_shapes=[
            pltpu.VMEM((atoms, PAD, LANES), jnp.bfloat16),
            pltpu.VMEM((frame, LANES, GROUP * PAD), jnp.float32),
        ],
        compiler_params=pltpu.CompilerParams(vmem_limit_bytes=20 * MIB),
        name="rotate_edges",
    )(slots, neighbour, *pieces, wigner)


def convolve_kernel(zero_shape, one_shape, x_ref, *refs):
    xs = 4
    column_refs = refs[:xs]
    rotated_ref, wigner_ref, out_ref, zero32, one32, zero16, real16, imag16, message, total = refs[xs:]
    zero_rows, zero_width = zero_shape
    parts, one_rows, one_width = one_shape
    ys = column_refs[0].shape[0]
    zero_tiles, one_tiles = zero_width // LANES, one_width // LANES
    for k in range(xs):
        place = (x_ref[1] + k) % xs
        for y in range(ys):
            g = (x_ref[0] + y) % ys * xs + place
            for i in range(zero_rows // 8):
                at = pl.multiple_of(g * zero_rows + 8 * i, 8)
                for t in range(zero_tiles):
                    zero32[pl.ds(at, 8), t * LANES : (t + 1) * LANES] = column_refs[k][
                        y, i * zero_tiles + t
                    ].astype(jnp.float32)
            first = zero_rows // 8 * zero_tiles
            for p in range(parts):
                for i in range(one_rows // 8):
                    at = pl.multiple_of(g * one_rows + 8 * i, 8)
                    for t in range(one_tiles):
                        one32[p, pl.ds(at, 8), t * LANES : (t + 1) * LANES] = column_refs[k][
                            y, first + (p * (one_rows // 8) + i) * one_tiles + t
                        ].astype(jnp.float32)
    zero16[...] = zero32[...].astype(jnp.bfloat16)
    real16[...] = one32[0].astype(jnp.bfloat16)
    imag16[...] = one32[1].astype(jnp.bfloat16)

    edges = rotated_ref.shape[0]
    frame = wigner_ref.shape[0]
    atoms = edges // NEIGH
    side = LMAX * LANES
    near = zero_width

    def times(a, b_ref):
        return lax.dot_general(a, b_ref[...], (((1,), (1,)), ((), ())), preferred_element_type=jnp.float32)

    rows = edges // 3
    for b in range(3):
        span = slice(b * rows, (b + 1) * rows)
        message[span, :near] = times(rotated_ref[span, :near], zero16).astype(jnp.bfloat16)
        plus = rotated_ref[span, near : near + side]
        minus = rotated_ref[span, near + side :]
        message[span, near : near + side] = (times(plus, real16) - times(minus, imag16)).astype(jnp.bfloat16)
        message[span, near + side :] = (times(plus, imag16) + times(minus, real16)).astype(jnp.bfloat16)

    total[...] = jnp.zeros_like(total)
    lane = lax.broadcasted_iota(jnp.int32, (PAD, LANES), 1)
    for b in range(edges // LANES):
        low = b * LANES
        first_atom = low // NEIGH
        last_atom = (low + LANES - 1) // NEIGH
        part = None
        for r0 in range(0, frame, 2):
            pair = [r for r in (r0, r0 + 1) if r < frame]
            left = []
            for r in pair:
                w = wigner_ref[r, :, low : low + LANES]
                picks = []
                for a in range(first_atom, last_atom + 1):
                    inside = (lane + low >= a * NEIGH) & (lane + low < (a + 1) * NEIGH)
                    picks.append(jnp.where(inside, w, jnp.zeros_like(w)))
                left.append(jnp.concatenate(picks, axis=0))
            lhs = jnp.concatenate(left, axis=1)
            rhs = jnp.concatenate(
                [message[low : low + LANES, r * LANES : (r + 1) * LANES] for r in pair], axis=0
            )
            got = lax.dot_general(lhs, rhs, (((1,), (0,)), ((), ())), preferred_element_type=jnp.float32)
            part = got if part is None else part + got
        window = slice(first_atom * PAD, (last_atom + 1) * PAD)
        total[window, :] = total[window, :] + part
    for k in range(out_ref.shape[0]):
        row = total[pl.ds(k, atoms, stride=PAD), :]
        out_ref[k] = (row * (1.0 / math.sqrt(NEIGH))).astype(out_ref.dtype)


def convolve(x, columns, rotated, wigner, zero_shape, one_shape, harmonics):
    edges = rotated.shape[0]
    atoms = edges // NEIGH
    parts, _, one_width = one_shape
    total_zero, total_one = zero_shape[1], one_width
    return pl.pallas_call(
        lambda *refs: convolve_kernel(zero_shape, one_shape, *refs),
        out_shape=jax.ShapeDtypeStruct((harmonics, atoms, LANES), jnp.bfloat16),
        in_specs=[pl.BlockSpec(memory_space=pltpu.SMEM)]
        + [pl.BlockSpec(memory_space=pltpu.VMEM)] * (len(columns) + 2),
        out_specs=pl.BlockSpec(memory_space=pltpu.VMEM),
        scratch_shapes=[
            pltpu.VMEM((total_zero, total_zero), jnp.float32),
            pltpu.VMEM((parts, total_one, total_one), jnp.float32),
            pltpu.VMEM((total_zero, total_zero), jnp.bfloat16),
            pltpu.VMEM((total_one, total_one), jnp.bfloat16),
            pltpu.VMEM((total_one, total_one), jnp.bfloat16),
            pltpu.VMEM((edges, rotated.shape[1]), jnp.bfloat16),
            pltpu.VMEM((atoms * PAD, LANES), jnp.float32),
        ],
        compiler_params=pltpu.CompilerParams(vmem_limit_bytes=28 * MIB),
        name="convolve_edges",
    )(x, *columns, rotated, wigner)


def added(a, b):
    return (a.astype(jnp.float32) + b.astype(jnp.float32)).astype(jnp.bfloat16)


def shards(
    node_features,
    atom_slot,
    neighbour,
    pad_mask,
    envelope,
    wigner_rows,
    mix_table,
    zero_weight,
    one_weight,
):
    yh, z, c = (lax.axis_index(a) for a in SYS)
    y, x = (lax.axis_index(a) for a in GRAPH)
    ys, xs = lax.axis_size("yl"), lax.axis_size("x")
    zero_rows, zero_width = zero_weight.shape[1:]
    one_rows, parts, one_width = one_weight.shape[1:]
    harmonics = wigner_rows.shape[2]
    packed = jnp.concatenate(
        [
            lane_tiles(zero_weight[0]),
            lane_tiles(one_weight[0].transpose(1, 0, 2).reshape(parts * one_rows, one_width)),
        ],
        axis=0,
    )
    chunks = copies_from_all(packed, "z")
    mine = node_features[0].reshape(-1, LANES)
    line = [mine]
    for k in range(1, ys):
        line.append(turned(mine, "yl", -k))
    line = jnp.concatenate(line, axis=0)
    plane = [line]
    for k in range(1, xs):
        plane.append(turned(line, "x", -k))

    edge_gate = envelope[0] * pad_mask[0].astype(jnp.float32)
    padding = ((0, 0), (0, PAD - harmonics), (0, 0))
    wigner = jnp.pad(wigner_rows[0], padding)
    gated = jnp.pad((wigner_rows[0].astype(jnp.float32) * edge_gate).astype(jnp.bfloat16), padding)
    slots = atom_slot[0]
    atoms = node_features.shape[1]
    slots = (
        (slots // atoms - x) % xs * (ys * atoms) + (slots // (xs * atoms) - y) % ys * atoms + slots % atoms
    )
    edges_from = neighbour[0]
    zs = lax.axis_size("z")
    table = mix_table.reshape(2, zs, 2, 2, zs, 2)
    table = lax.dynamic_slice(table, (0, z, 0, yh, 0, c), (2, 1, 2, 1, zs, 1)).reshape(2, 2, zs)
    table = jnp.where(yh == 0, table, table[::-1])
    factors = jnp.where(c == 0, table, table[:, ::-1]).reshape(4, zs)
    there = jnp.stack([y, x])
    wigner, gated, slots, edges_from, chunks, factors, there = lax.optimization_barrier(
        (wigner, gated, slots, edges_from, chunks, factors, there)
    )
    send, other, own = partial_sums(factors, chunks)
    swapped = turned(send, "c", 1)
    outgoing = added(other, swapped[1])
    arrived = turned(outgoing, "yh", 1)
    pieces = [p.reshape(-1, harmonics, LANES) for p in plane]
    arrived, pieces = lax.optimization_barrier((arrived, pieces))
    merged = added(added(own, swapped[0]), arrived)
    column = [merged]
    for k in range(1, ys):
        column.append(turned(merged, "yl", -k))
    column = jnp.stack(column)
    columns = [column]
    for k in range(1, xs):
        columns.append(turned(column, "x", -k))
    rotated = rotate(slots, edges_from, pieces, wigner)
    update = convolve(
        there,
        [m.reshape(ys, -1, 8, LANES) for m in columns],
        rotated,
        gated,
        (zero_rows, zero_width),
        (parts, one_rows, one_width),
        harmonics,
    )
    return update.transpose(1, 0, 2)[None]


def solution(mesh):
    finer = Mesh(mesh.devices.reshape(2, 8, 2, 4, 4), SYS + GRAPH)
    return jax.shard_map(
        shards,
        mesh=finer,
        in_specs=(
            P(SYS, GRAPH, None, None),
            P(SYS, None),
            P(SYS, GRAPH),
            P(SYS, GRAPH),
            P(SYS, GRAPH),
            P(SYS, None, None, GRAPH),
            P(),
            P(SYS, GRAPH, None),
            P(SYS, GRAPH, None, None),
        ),
        out_specs=P(SYS, GRAPH, None, None),
        check_vma=False,
    )
```

time: 232 us -> 141 us (0.61)
  the two profiles are of different devices: /device:TPU:6 before, /device:TPU:1 now
where the time goes in v1:
time: 141 us; the launch traced here: 140 us
  starting transfers between devices  54.3 us (39%)
  waiting for transfers between devices  52 us (37%)
  Pallas kernels  15.4 us (11%)
  local copies, waits for them, and re-layouts  14.9 us (11%)
  other arithmetic  3.07 us (2%)
    ppermute x14, starting transfers between devices, turned(): lax.ppermute(value, axis, [(i, (i + by) % size) for i in range(size)])  44.1 us
    ppermute x14, waiting for transfers between devices, turned(): lax.ppermute(value, axis, [(i, (i + by) % size) for i in range(size)])  28.2 us
    all_to_all x1, waiting for transfers between devices, copies_from_all(): return lax.all_to_all(spread, axis, 0, 0, tiled=True)  23.8 us
    all_to_all x1, starting transfers between devices, copies_from_all(): return lax.all_to_all(spread, axis, 0, 0, tiled=True)  10.2 us
    pallas_call x1, Pallas kernels, rotate(): pl.pallas_call(rotate_kernel, out_shape=jax.ShapeDtypeStruct((edges, fram...  8.07 us
    unnamed x24, local copies, waits for them, and re-layouts  6.35 us
    pallas_call x1, Pallas kernels, convolve(): pl.pallas_call(lambda *refs: convolve_kernel(zero_shape, one_shape, *refs...  6.2 us
    reshape x4, local copies, waits for them, and re-layouts, shards(): pieces = [p.reshape(-1, harmonics, LANES) for p in plane]  5.37 us
  transfers between devices with their start and end apart: 15, of which 6 were waited for; matrix products, arithmetic and copies ran while one was open for 10% of the time, Pallas kernels for 7%

profile of v1, /device:TPU:1, one launch (start us, length us, event | category | flops | bytes accessed | tf_op | source)
XLA Modules:
  0.0 140.0 jit_solution(18304637324532101314)
XLA Ops:
  0.0 0.9 copy.17
  0.9 0.0 copy-start.2
  1.0 6.2 %collective-permute-start.2 = (bf16[400,128]{1,0:T(8,128)(2,1)S(1)}, bf16[400,128]{1,0:T(8,128)(2,1)S(1)}, u32[]{:S(2)}, u32[]{:S(2)}) collective-permute-start(bf16[400,128]{1,0:T(8,128)(2,1)S(1)} %reshape_squeeze.7), channel_id=1, source_target_pairs={{0,12},{4,0},{8,4},{12,8},{1,13},{5,1},{9,5},{13,9},{2,14},{6,2},{... | collective-permute-start | bytes 307208 | tf_op jit(solution)/shard_map/ppermute | solution.py:24
  7.2 1.9 %collective-permute-start.3 = (bf16[400,128]{1,0:T(8,128)(2,1)S(1)}, bf16[400,128]{1,0:T(8,128)(2,1)}, u32[]{:S(2)}, u32[]{:S(2)}) collective-permute-start(bf16[400,128]{1,0:T(8,128)(2,1)S(1)} %reshape_squeeze.7), channel_id=1, source_target_pairs={{0,8},{4,12},{8,0},{12,4},{1,9},{5,13},{9,1},{13,5},{2,10},{6,14},... | collective-permute-start | bytes 307208 | tf_op jit(solution)/shard_map/ppermute | solution.py:24
  9.1 2.4 %collective-permute-start.4 = (bf16[400,128]{1,0:T(8,128)(2,1)S(1)}, bf16[400,128]{1,0:T(8,128)(2,1)}, u32[]{:S(2)}, u32[]{:S(2)}) collective-permute-start(bf16[400,128]{1,0:T(8,128)(2,1)S(1)} %reshape_squeeze.7), channel_id=1, source_target_pairs={{0,4},{4,8},{8,12},{12,0},{1,5},{5,9},{9,13},{13,1},{2,6},{6,10},{... | collective-permute-start | bytes 307208 | tf_op jit(solution)/shard_map/ppermute | solution.py:24
  11.5 0.9 copy.16
  12.3 0.8 pad_maximum_fusion.2
  13.2 1.1 broadcast_in_dim.4
  14.3 10.2 %all-to-all-start = ((bf16[8,456,128]{2,1,0:T(8,128)(2,1)}), bf16[8,456,128]{2,1,0:T(8,128)(2,1)S(1)}, u32[]{:S(2)}, u32[]{:S(2)}) async-start(bf16[8,456,128]{2,1,0:T(8,128)(2,1)} %broadcast_in_dim.4), calls=%async_computation | async-start | bytes 1867776 | tf_op jit(solution)/shard_map/all_to_all | solution.py:30
  24.4 0.0 copy-done.4
  24.4 0.2 reshape.76
  24.6 0.2 dynamic-slice_reduce_fusion
  24.8 0.0 copy-done.2
  24.8 0.2 copy.21
  25.0 0.0 copy-done.6
  25.0 0.2 multiply_convert_fusion
  25.2 0.0 copy-start.5
  25.2 0.0 copy-start.8
  25.2 0.1 pad.8.refs_6_
  25.3 0.1 pad.7.refs_4_
  25.4 0.5 copy-done.5
  25.9 0.7 constant_dynamic-update-slice_fusion.3
  26.6 0.1 pad_add_fusion.refs_0_
  26.7 0.0 collective-permute-done.2
  26.7 0.6 constant_dynamic-update-slice_fusion.2
  27.3 23.8 %all-to-all-done = bf16[8,456,128]{2,1,0:T(8,128)(2,1)S(1)} async-done(((bf16[8,456,128]{2,1,0:T(8,128)(2,1)}), bf16[8,456,128]{2,1,0:T(8,128)(2,1)S(1)}, u32[]{:S(2)}, u32[]{:S(2)}) %all-to-all-start) | async-done | bytes 933920 | tf_op jit(solution)/shard_map/all_to_all | solution.py:30
  51.2 1.1 merge_experts.1
  52.3 2.4 %collective-permute-start = (bf16[2,456,128]{2,1,0:T(8,128)(2,1)S(1)}, bf16[2,456,128]{2,1,0:T(8,128)(2,1)S(1)}, u32[]{:S(2)}, u32[]{:S(2)}) collective-permute-start(bf16[2,456,128]{2,1,0:T(8,128)(2,1)S(1)} %bitcast.60), channel_id=1, source_target_pairs={{0,16},{16,0},{1,17},{17,1},{2,18},{18,2},{3,19},{19,3},{4,20},{20... | collective-permute-start | bytes 700424 | tf_op jit(solution)/shard_map/ppermute | solution.py:24
  54.7 0.0 collective-permute-done.3
  54.7 1.5 %constant_dynamic-update-slice_fusion.1 = bf16[1600,128]{1,0:T(8,128)(2,1)} fusion(bf16[1600,128]{1,0:T(8,128)(2,1)} %constant_dynamic-update-slice_fusion.2, bf16[400,128]{1,0:T(8,128)(2,1)} %collective-permute-done.3), kind=kLoop, calls=%fused_computation.14 | loop fusion | bytes 204800
  56.3 0.0 collective-permute-done.4
  56.3 1.5 %constant_dynamic-update-slice_fusion = bf16[1600,128]{1,0:T(8,128)(2,1)} fusion(bf16[1600,128]{1,0:T(8,128)(2,1)} %constant_dynamic-update-slice_fusion.1, bf16[400,128]{1,0:T(8,128)(2,1)} %collective-permute-done.4), kind=kLoop, calls=%fused_computation.13 | loop fusion | bytes 204800 | tf_op jit(solution)/shard_map/concatenate | solution.py:284
  57.8 4.4 %collective-permute-start.5 = (bf16[1600,128]{1,0:T(8,128)(2,1)}, bf16[1600,128]{1,0:T(8,128)(2,1)}, u32[]{:S(2)}, u32[]{:S(2)}) collective-permute-start(bf16[1600,128]{1,0:T(8,128)(2,1)} %constant_dynamic-update-slice_fusion), channel_id=1, source_target_pairs={{0,3},{1,0},{2,1},{3,2},{4,7},{5,4},{6,5},{7,6},{8,11},{9,8},{10,9... | collective-permute-start | bytes 1228808 | tf_op jit(solution)/shard_map/ppermute | solution.py:24
  62.2 2.4 %collective-permute-start.6 = (bf16[1600,128]{1,0:T(8,128)(2,1)}, bf16[1600,128]{1,0:T(8,128)(2,1)}, u32[]{:S(2)}, u32[]{:S(2)}) collective-permute-start(bf16[1600,128]{1,0:T(8,128)(2,1)} %constant_dynamic-update-slice_fusion), channel_id=1, source_target_pairs={{0,2},{1,3},{2,0},{3,1},{4,6},{5,7},{6,4},{7,5},{8,10},{9,11},{10,... | collective-permute-start | bytes 1228808 | tf_op jit(solution)/shard_map/ppermute | solution.py:24
  64.6 2.5 %collective-permute-start.7 = (bf16[1600,128]{1,0:T(8,128)(2,1)}, bf16[1600,128]{1,0:T(8,128)(2,1)}, u32[]{:S(2)}, u32[]{:S(2)}) collective-permute-start(bf16[1600,128]{1,0:T(8,128)(2,1)} %constant_dynamic-update-slice_fusion), channel_id=1, source_target_pairs={{0,1},{1,2},{2,3},{3,0},{4,5},{5,6},{6,7},{7,4},{8,9},{9,10},{10,1... | collective-permute-start | bytes 1228808 | tf_op jit(solution)/shard_map/ppermute | solution.py:24
  67.1 0.0 collective-permute-done
  67.2 0.7 fusion
  67.9 5.6 %collective-permute-start.1 = (bf16[456,128]{1,0:T(8,128)(2,1)}, bf16[456,128]{1,0:T(8,128)(2,1)}, u32[]{:S(2)}, u32[]{:S(2)}) collective-permute-start(bf16[456,128]{1,0:T(8,128)(2,1)} %fusion), channel_id=1, source_target_pairs={{0,256},{256,0},{1,257},{257,1},{2,258},{258,2},{3,259},{259,3},{4... | collective-permute-start | bytes 350216 | tf_op jit(solution)/shard_map/ppermute | solution.py:24
  73.5 1.1 reshape.81.refs_0_
  74.7 5.2 %collective-permute-done.5 = bf16[1600,128]{1,0:T(8,128)(2,1)} collective-permute-done((bf16[1600,128]{1,0:T(8,128)(2,1)}, bf16[1600,128]{1,0:T(8,128)(2,1)}, u32[]{:S(2)}, u32[]{:S(2)}) %collective-permute-start.5) | collective-permute-done | bytes 409632 | tf_op jit(solution)/shard_map/ppermute | solution.py:24
  79.9 1.1 reshape.82.refs_1_
  81.1 0.0 collective-permute-done.6
  81.1 1.1 reshape.83.refs_2_
  82.2 3.8 %collective-permute-done.7 = bf16[1600,128]{1,0:T(8,128)(2,1)} collective-permute-done((bf16[1600,128]{1,0:T(8,128)(2,1)}, bf16[1600,128]{1,0:T(8,128)(2,1)}, u32[]{:S(2)}, u32[]{:S(2)}) %collective-permute-start.7) | collective-permute-done | bytes 409632 | tf_op jit(solution)/shard_map/ppermute | solution.py:24
  86.1 1.9 %reshape.84.refs_3_ = bf16[64,25,128]{2,1,0:T(8,128)(2,1)} reshape(bf16[1600,128]{1,0:T(8,128)(2,1)} %collective-permute-done.7) | data formatting | bytes 819200 | tf_op jit(solution)/shard_map/reshape | solution.py:312
  88.0 0.0 collective-permute-done.1
  88.0 1.1 add_convert_fusion
  89.1 4.7 %collective-permute-start.8 = (bf16[456,128]{1,0:T(8,128)(2,1)S(1)}, bf16[456,128]{1,0:T(8,128)(2,1)S(1)}, u32[]{:S(2)}, u32[]{:S(2)}) collective-permute-start(bf16[456,128]{1,0:T(8,128)(2,1)S(1)} %add_convert_fusion), channel_id=1, source_target_pairs={{0,12},{4,0},{8,4},{12,8},{1,13},{5,1},{9,5},{13,9},{2,14},{6,2},{... | collective-permute-start | bytes 350216 | tf_op jit(solution)/shard_map/ppermute | solution.py:24
  93.8 2.5 %collective-permute-start.9 = (bf16[456,128]{1,0:T(8,128)(2,1)S(1)}, bf16[456,128]{1,0:T(8,128)(2,1)S(1)}, u32[]{:S(2)}, u32[]{:S(2)}) collective-permute-start(bf16[456,128]{1,0:T(8,128)(2,1)S(1)} %add_convert_fusion), channel_id=1, source_target_pairs={{0,8},{4,12},{8,0},{12,4},{1,9},{5,13},{9,1},{13,5},{2,10},{6,14},... | collective-permute-start | bytes 350216 | tf_op jit(solution)/shard_map/ppermute | solution.py:24
  96.3 1.9 %collective-permute-start.10 = (bf16[456,128]{1,0:T(8,128)(2,1)S(1)}, bf16[456,128]{1,0:T(8,128)(2,1)S(1)}, u32[]{:S(2)}, u32[]{:S(2)}) collective-permute-start(bf16[456,128]{1,0:T(8,128)(2,1)S(1)} %add_convert_fusion), channel_id=1, source_target_pairs={{0,4},{4,8},{8,12},{12,0},{1,5},{5,9},{9,13},{13,1},{2,6},{6,10},{... | collective-permute-start | bytes 350216 | tf_op jit(solution)/shard_map/ppermute | solution.py:24
  98.2 0.0 collective-permute-done.8
  98.2 7.6 %collective-permute-done.9 = bf16[456,128]{1,0:T(8,128)(2,1)S(1)} collective-permute-done((bf16[456,128]{1,0:T(8,128)(2,1)S(1)}, bf16[456,128]{1,0:T(8,128)(2,1)S(1)}, u32[]{:S(2)}, u32[]{:S(2)}) %collective-permute-start.9) | collective-permute-done | bytes 116768 | tf_op jit(solution)/shard_map/ppermute | solution.py:24
  105.8 0.0 collective-permute-done.10
  105.8 0.1 pad_maximum_fusion.1
  105.9 1.9 %collective-permute-start.11 = (bf16[4,456,128]{2,1,0:T(8,128)(2,1)S(1)}, bf16[4,456,128]{2,1,0:T(8,128)(2,1)S(1)}, u32[]{:S(2)}, u32[]{:S(2)}) collective-permute-start(bf16[4,456,128]{2,1,0:T(8,128)(2,1)S(1)} %pad_maximum_fusion.1), channel_id=1, source_target_pairs={{0,3},{1,0},{2,1},{3,2},{4,7},{5,4},{6,5},{7,6},{8,11},{9,8},{10,9... | collective-permute-start | bytes 1400840 | tf_op jit(solution)/shard_map/ppermute | solution.py:24
  107.8 2.4 %collective-permute-start.12 = (bf16[4,456,128]{2,1,0:T(8,128)(2,1)S(1)}, bf16[4,456,128]{2,1,0:T(8,128)(2,1)S(1)}, u32[]{:S(2)}, u32[]{:S(2)}) collective-permute-start(bf16[4,456,128]{2,1,0:T(8,128)(2,1)S(1)} %pad_maximum_fusion.1), channel_id=1, source_target_pairs={{0,2},{1,3},{2,0},{3,1},{4,6},{5,7},{6,4},{7,5},{8,10},{9,11},{10,... | collective-permute-start | bytes 1400840 | tf_op jit(solution)/shard_map/ppermute | solution.py:24
  110.3 2.9 %collective-permute-start.13 = (bf16[4,456,128]{2,1,0:T(8,128)(2,1)S(1)}, bf16[4,456,128]{2,1,0:T(8,128)(2,1)S(1)}, u32[]{:S(2)}, u32[]{:S(2)}) collective-permute-start(bf16[4,456,128]{2,1,0:T(8,128)(2,1)S(1)} %pad_maximum_fusion.1), channel_id=1, source_target_pairs={{0,1},{1,2},{2,3},{3,0},{4,5},{5,6},{6,7},{7,4},{8,9},{9,10},{10,1... | collective-permute-start | bytes 1400840 | tf_op jit(solution)/shard_map/ppermute | solution.py:24
  113.1 1.0 copy-done
  114.2 8.1 %rotate_edges.1.refs_5_ = bf16[1152,1664]{1,0:T(8,128)(2,1)S(1)} custom-call(s32[256]{0:T(256)S(1)} %fusion.4.slot_ref, s32[1152]{0:T(1024)S(1)} %reduce.1.neighbour_ref, bf16[64,25,128]{2,1,0:T(8,128)(2,1)S(1)} %reshape.81.refs_0_, bf16[64,25,128]{2,1,0:T(8,128)(2,1)S(1)} %reshape.82.refs_1_, bf16[64,25,128]{2,1,0:T(8,128)(2,1)S(1)} %reshape.83.refs_2_, ...), custom_call_target="tpu_custom_call" | custom-call | tf_op jit(solution)/shard_map/rotate_edges/pallas_call | solution.py:130
  122.2 0.1 pad_maximum_fusion.refs_1_
  122.3 0.0 collective-permute-done.11
  122.3 0.6 collective-permute-done.12
  122.9 10.9 %collective-permute-done.13 = bf16[4,456,128]{2,1,0:T(8,128)(2,1)S(1)} collective-permute-done((bf16[4,456,128]{2,1,0:T(8,128)(2,1)S(1)}, bf16[4,456,128]{2,1,0:T(8,128)(2,1)S(1)}, u32[]{:S(2)}, u32[]{:S(2)}) %collective-permute-start.13) | collective-permute-done | bytes 466976 | tf_op jit(solution)/shard_map/ppermute | solution.py:24
  133.8 6.2 %convolve_edges.1 = bf16[25,16,128]{2,1,0:T(8,128)(2,1)} custom-call(s32[2]{0:T(128)S(1)} %pad_add_fusion.refs_0_, bf16[4,57,8,128]{3,2,1,0:T(8,128)(2,1)S(1)} %pad_maximum_fusion.refs_1_, bf16[4,57,8,128]{3,2,1,0:T(8,128)(2,1)S(1)} %bitcast.56, bf16[4,57,8,128]{3,2,1,0:T(8,128)(2,1)S(1)} %bitcast.57, bf16[4,57,8,128]{3,2,1,0:T(8,128)(2,1)S(1)} %bitcast.58, ...), custom_call_target="tpu_custom_call" | custom-call | tf_op jit(solution)/shard_map/convolve_edges/pallas_call | solution.py:231
  (17 shorter events, 0.2 us)
Async XLA Ops:
  0.0 24.4 %copy-start.4 = (f32[32,32]{1,0:T(8,128)S(1)}, f32[32,32]{1,0:T(8,128)}, u32[]{:S(2)}) copy-start(f32[32,32]{1,0:T(8,128)} %param.15) | copy-start | bytes 12292
  0.9 23.9 %copy-start.2 = (bf16[1,13,25,1152]{3,1,2,0:T(8,128)(2,1)S(1)}, bf16[1,13,25,1152]{3,1,2,0:T(8,128)(2,1)}, u32[]{:S(2)}) copy-start(bf16[1,13,25,1152]{3,1,2,0:T(8,128)(2,1)} %param.14) | copy-start | bytes 2246404
  1.0 25.7 %collective-permute-start.2 = (bf16[400,128]{1,0:T(8,128)(2,1)S(1)}, bf16[400,128]{1,0:T(8,128)(2,1)S(1)}, u32[]{:S(2)}, u32[]{:S(2)}) collective-permute-start(bf16[400,128]{1,0:T(8,128)(2,1)S(1)} %reshape_squeeze.7), channel_id=1, source_target_pairs={{0,12},{4,0},{8,4},{12,8},{1,13},{5,1},{9,5},{13,9},{2,14},{6,2},{... | collective-permute-start | bytes 307208 | tf_op jit(solution)/shard_map/ppermute | solution.py:24
  7.2 47.5 %collective-permute-start.3 = (bf16[400,128]{1,0:T(8,128)(2,1)S(1)}, bf16[400,128]{1,0:T(8,128)(2,1)}, u32[]{:S(2)}, u32[]{:S(2)}) collective-permute-start(bf16[400,128]{1,0:T(8,128)(2,1)S(1)} %reshape_squeeze.7), channel_id=1, source_target_pairs={{0,8},{4,12},{8,0},{12,4},{1,9},{5,13},{9,1},{13,5},{2,10},{6,14},... | collective-permute-start | bytes 307208 | tf_op jit(solution)/shard_map/ppermute | solution.py:24
  9.1 47.1 %collective-permute-start.4 = (bf16[400,128]{1,0:T(8,128)(2,1)S(1)}, bf16[400,128]{1,0:T(8,128)(2,1)}, u32[]{:S(2)}, u32[]{:S(2)}) collective-permute-start(bf16[400,128]{1,0:T(8,128)(2,1)S(1)} %reshape_squeeze.7), channel_id=1, source_target_pairs={{0,4},{4,8},{8,12},{12,0},{1,5},{5,9},{9,13},{13,1},{2,6},{6,10},{... | collective-permute-start | bytes 307208 | tf_op jit(solution)/shard_map/ppermute | solution.py:24
  14.3 10.7 %copy-start.6 = (f32[1,1152]{1,0:T(1,128)S(1)}, f32[1,1152]{1,0:T(1,128)}, u32[]{:S(2)}) copy-start(f32[1,1152]{1,0:T(1,128)} %param.13) | copy-start | bytes 13828
  14.3 10.7 %copy-start.7 = (s32[1,1152]{1,0:T(1,128)S(1)}, s32[1,1152]{1,0:T(1,128)}, u32[]{:S(2)}) copy-start(s32[1,1152]{1,0:T(1,128)} %param.12) | copy-start | bytes 13828
  14.3 36.9 %all-to-all-start = ((bf16[8,456,128]{2,1,0:T(8,128)(2,1)}), bf16[8,456,128]{2,1,0:T(8,128)(2,1)S(1)}, u32[]{:S(2)}, u32[]{:S(2)}) async-start(bf16[8,456,128]{2,1,0:T(8,128)(2,1)} %broadcast_in_dim.4), calls=%async_computation | async-start | bytes 1867776 | tf_op jit(solution)/shard_map/all_to_all | solution.py:30
  25.2 0.7 copy-start.5
  25.2 1.4 copy-start.8
  52.3 15.6 %copy-start.1 = (bf16[57,8,128]{2,1,0:T(8,128)(2,1)}, bf16[57,8,128]{2,1,0:T(8,128)(2,1)S(1)}, u32[]{:S(2)}) copy-start(bf16[57,8,128]{2,1,0:T(8,128)(2,1)S(1)} %get-tuple-element.23) | copy-start | bytes 350212
  52.3 14.9 %collective-permute-start = (bf16[2,456,128]{2,1,0:T(8,128)(2,1)S(1)}, bf16[2,456,128]{2,1,0:T(8,128)(2,1)S(1)}, u32[]{:S(2)}, u32[]{:S(2)}) collective-permute-start(bf16[2,456,128]{2,1,0:T(8,128)(2,1)S(1)} %bitcast.60), channel_id=1, source_target_pairs={{0,16},{16,0},{1,17},{17,1},{2,18},{18,2},{3,19},{19,3},{4,20},{20... | collective-permute-start | bytes 700424 | tf_op jit(solution)/shard_map/ppermute | solution.py:24
  57.8 22.1 %collective-permute-start.5 = (bf16[1600,128]{1,0:T(8,128)(2,1)}, bf16[1600,128]{1,0:T(8,128)(2,1)}, u32[]{:S(2)}, u32[]{:S(2)}) collective-permute-start(bf16[1600,128]{1,0:T(8,128)(2,1)} %constant_dynamic-update-slice_fusion), channel_id=1, source_target_pairs={{0,3},{1,0},{2,1},{3,2},{4,7},{5,4},{6,5},{7,6},{8,11},{9,8},{10,9... | collective-permute-start | bytes 1228808 | tf_op jit(solution)/shard_map/ppermute | solution.py:24
  62.2 18.9 %collective-permute-start.6 = (bf16[1600,128]{1,0:T(8,128)(2,1)}, bf16[1600,128]{1,0:T(8,128)(2,1)}, u32[]{:S(2)}, u32[]{:S(2)}) collective-permute-start(bf16[1600,128]{1,0:T(8,128)(2,1)} %constant_dynamic-update-slice_fusion), channel_id=1, source_target_pairs={{0,2},{1,3},{2,0},{3,1},{4,6},{5,7},{6,4},{7,5},{8,10},{9,11},{10,... | collective-permute-start | bytes 1228808 | tf_op jit(solution)/shard_map/ppermute | solution.py:24
  64.6 21.4 %collective-permute-start.7 = (bf16[1600,128]{1,0:T(8,128)(2,1)}, bf16[1600,128]{1,0:T(8,128)(2,1)}, u32[]{:S(2)}, u32[]{:S(2)}) collective-permute-start(bf16[1600,128]{1,0:T(8,128)(2,1)} %constant_dynamic-update-slice_fusion), channel_id=1, source_target_pairs={{0,1},{1,2},{2,3},{3,0},{4,5},{5,6},{6,7},{7,4},{8,9},{9,10},{10,1... | collective-permute-start | bytes 1228808 | tf_op jit(solution)/shard_map/ppermute | solution.py:24
  67.2 13.9 %copy-start.3 = (bf16[2,456,128]{2,1,0:T(8,128)(2,1)}, bf16[2,456,128]{2,1,0:T(8,128)(2,1)S(1)}, u32[]{:S(2)}) copy-start(bf16[2,456,128]{2,1,0:T(8,128)(2,1)S(1)} %collective-permute-done) | copy-start | bytes 700420
  67.9 20.1 %collective-permute-start.1 = (bf16[456,128]{1,0:T(8,128)(2,1)}, bf16[456,128]{1,0:T(8,128)(2,1)}, u32[]{:S(2)}, u32[]{:S(2)}) collective-permute-start(bf16[456,128]{1,0:T(8,128)(2,1)} %fusion), channel_id=1, source_target_pairs={{0,256},{256,0},{1,257},{257,1},{2,258},{258,2},{3,259},{259,3},{4... | collective-permute-start | bytes 350216 | tf_op jit(solution)/shard_map/ppermute | solution.py:24
  89.1 9.1 %collective-permute-start.8 = (bf16[456,128]{1,0:T(8,128)(2,1)S(1)}, bf16[456,128]{1,0:T(8,128)(2,1)S(1)}, u32[]{:S(2)}, u32[]{:S(2)}) collective-permute-start(bf16[456,128]{1,0:T(8,128)(2,1)S(1)} %add_convert_fusion), channel_id=1, source_target_pairs={{0,12},{4,0},{8,4},{12,8},{1,13},{5,1},{9,5},{13,9},{2,14},{6,2},{... | collective-permute-start | bytes 350216 | tf_op jit(solution)/shard_map/ppermute | solution.py:24
  93.8 12.0 %collective-permute-start.9 = (bf16[456,128]{1,0:T(8,128)(2,1)S(1)}, bf16[456,128]{1,0:T(8,128)(2,1)S(1)}, u32[]{:S(2)}, u32[]{:S(2)}) collective-permute-start(bf16[456,128]{1,0:T(8,128)(2,1)S(1)} %add_convert_fusion), channel_id=1, source_target_pairs={{0,8},{4,12},{8,0},{12,4},{1,9},{5,13},{9,1},{13,5},{2,10},{6,14},... | collective-permute-start | bytes 350216 | tf_op jit(solution)/shard_map/ppermute | solution.py:24
  96.3 9.5 %collective-permute-start.10 = (bf16[456,128]{1,0:T(8,128)(2,1)S(1)}, bf16[456,128]{1,0:T(8,128)(2,1)S(1)}, u32[]{:S(2)}, u32[]{:S(2)}) collective-permute-start(bf16[456,128]{1,0:T(8,128)(2,1)S(1)} %add_convert_fusion), channel_id=1, source_target_pairs={{0,4},{4,8},{8,12},{12,0},{1,5},{5,9},{9,13},{13,1},{2,6},{6,10},{... | collective-permute-start | bytes 350216 | tf_op jit(solution)/shard_map/ppermute | solution.py:24
  105.9 16.4 %collective-permute-start.11 = (bf16[4,456,128]{2,1,0:T(8,128)(2,1)S(1)}, bf16[4,456,128]{2,1,0:T(8,128)(2,1)S(1)}, u32[]{:S(2)}, u32[]{:S(2)}) collective-permute-start(bf16[4,456,128]{2,1,0:T(8,128)(2,1)S(1)} %pad_maximum_fusion.1), channel_id=1, source_target_pairs={{0,3},{1,0},{2,1},{3,2},{4,7},{5,4},{6,5},{7,6},{8,11},{9,8},{10,9... | collective-permute-start | bytes 1400840 | tf_op jit(solution)/shard_map/ppermute | solution.py:24
  107.8 15.1 %collective-permute-start.12 = (bf16[4,456,128]{2,1,0:T(8,128)(2,1)S(1)}, bf16[4,456,128]{2,1,0:T(8,128)(2,1)S(1)}, u32[]{:S(2)}, u32[]{:S(2)}) collective-permute-start(bf16[4,456,128]{2,1,0:T(8,128)(2,1)S(1)} %pad_maximum_fusion.1), channel_id=1, source_target_pairs={{0,2},{1,3},{2,0},{3,1},{4,6},{5,7},{6,4},{7,5},{8,10},{9,11},{10,... | collective-permute-start | bytes 1400840 | tf_op jit(solution)/shard_map/ppermute | solution.py:24
  110.3 23.6 %collective-permute-start.13 = (bf16[4,456,128]{2,1,0:T(8,128)(2,1)S(1)}, bf16[4,456,128]{2,1,0:T(8,128)(2,1)S(1)}, u32[]{:S(2)}, u32[]{:S(2)}) collective-permute-start(bf16[4,456,128]{2,1,0:T(8,128)(2,1)S(1)} %pad_maximum_fusion.1), channel_id=1, source_target_pairs={{0,1},{1,2},{2,3},{3,0},{4,5},{5,6},{6,7},{7,4},{8,9},{9,10},{10,1... | collective-permute-start | bytes 1400840 | tf_op jit(solution)/shard_map/ppermute | solution.py:24
  113.1 1.0 copy-start

commit v2 on v1

--- a/solution.py
+++ b/solution.py
@@ -16,6 +16,7 @@
 LANES = 128
 PAD = 32
 GROUP = 8
+FAR_FIRST = (2, 1, 3)
 MIB = 1024 * 1024
 
 
@@ -24,15 +25,49 @@
     return lax.ppermute(value, axis, [(i, (i + by) % size) for i in range(size)])
 
 
-def copies_from_all(value, axis):
-    size = math.prod(lax.axis_size(a) for a in axis) if isinstance(axis, tuple) else lax.axis_size(axis)
-    spread = jnp.broadcast_to(value[None], (size, *value.shape))
-    return lax.all_to_all(spread, axis, 0, 0, tiled=True)
-
-
-def lane_tiles(rows):
-    height, width = rows.shape
-    return rows.reshape(height // 8, 8, width // LANES, LANES).transpose(0, 2, 1, 3).reshape(-1, LANES)
+def spread_kernel(zero_hbm, one_hbm, out_ref, zero_ref, one_ref, sems):
+    loads = [
+        pltpu.make_async_copy(zero_hbm, zero_ref, sems.at[0]),
+        pltpu.make_async_copy(one_hbm, one_ref, sems.at[1]),
+    ]
+    for load in loads:
+        load.start()
+    for load in loads:
+        load.wait()
+    copies = out_ref.shape[0]
+    at = 0
+    for i in range(zero_ref.shape[0] // 8):
+        for t in range(zero_ref.shape[1] // LANES):
+            tile = zero_ref[8 * i : 8 * i + 8, t * LANES : (t + 1) * LANES]
+            for k in range(copies):
+                out_ref[k, at] = tile
+            at += 1
+    for p in range(one_ref.shape[1]):
+        for i in range(one_ref.shape[0] // 8):
+            for t in range(one_ref.shape[2] // LANES):
+                tile = one_ref[8 * i : 8 * i + 8, p, t * LANES : (t + 1) * LANES]
+                for k in range(copies):
+                    out_ref[k, at] = tile
+                at += 1
+
+
+def spread(zero, one, copies):
+    tiles = (zero.size + one.size) // (8 * LANES)
+    vmem = pl.BlockSpec(memory_space=pltpu.VMEM)
+    out = pl.pallas_call(
+        spread_kernel,
+        out_shape=jax.ShapeDtypeStruct((copies, tiles, 8, LANES), jnp.bfloat16),
+        in_specs=[pl.BlockSpec(memory_space=pltpu.HBM)] * 2,
+        out_specs=vmem,
+        scratch_shapes=[
+            pltpu.VMEM(zero.shape, zero.dtype),
+            pltpu.VMEM(one.shape, one.dtype),
+            pltpu.SemaphoreType.DMA((2,)),
+        ],
+        compiler_params=pltpu.CompilerParams(vmem_limit_bytes=8 * MIB),
+        name="spread_weights",
+    )(zero, one)
+    return out.reshape(copies, tiles * 8, LANES)
 
 
 def merge_kernel(factor_ref, chunk_ref, send_ref, other_ref, own_ref):
@@ -71,12 +106,20 @@
 
 def rotate_kernel(slot_ref, neighbour_ref, *refs):
     piece_refs = refs[:4]
-    wigner_ref, out_ref, feature_ref, spread_ref = refs[4:]
+    wigner_ref, out_ref, feature_ref, row_ref, spread_ref = refs[4:]
     frame = wigner_ref.shape[0]
-    atoms, harmonics = piece_refs[0].shape[:2]
-    for k, ref in enumerate(piece_refs):
-        feature_ref[k * atoms : (k + 1) * atoms, :harmonics] = ref[...]
-    feature_ref[:, harmonics:] = jnp.zeros_like(feature_ref[:, harmonics:])
+    runs, harmonics = piece_refs[0].shape[:2]
+    row_ref[:, 8 * harmonics :] = jnp.zeros_like(row_ref[:, 8 * harmonics :])
+
+    def eight_atoms(run, carry):
+        for k, ref in enumerate(piece_refs):
+            row_ref[k, : 8 * harmonics] = ref[run].astype(jnp.float32).reshape(8 * harmonics, LANES)
+            for a in range(8):
+                rows = row_ref[k, a * harmonics : a * harmonics + PAD]
+                feature_ref[(k * runs + run) * 8 + a] = rows.astype(jnp.bfloat16)
+        return carry
+
+    lax.fori_loop(0, runs, eight_atoms, 0)
     width = GROUP * PAD
     block = LANES
     column = lax.broadcasted_iota(jnp.int32, (PAD, width), 1)
@@ -126,7 +169,8 @@
 
 def rotate(slots, neighbour, pieces, wigner):
     frame, _, edges = wigner.shape
-    atoms = len(pieces) * pieces[0].shape[0]
+    runs, harmonics = pieces[0].shape[:2]
+    atoms = len(pieces) * runs * 8
     return pl.pallas_call(
         rotate_kernel,
         out_shape=jax.ShapeDtypeStruct((edges, frame * LANES), jnp.bfloat16),
@@ -138,6 +182,7 @@
         out_specs=pl.BlockSpec(memory_space=pltpu.VMEM),
         scratch_shapes=[
             pltpu.VMEM((atoms, PAD, LANES), jnp.bfloat16),
+            pltpu.VMEM((len(pieces), 8 * harmonics + 8, LANES), jnp.float32),
             pltpu.VMEM((frame, LANES, GROUP * PAD), jnp.float32),
         ],
         compiler_params=pltpu.CompilerParams(vmem_limit_bytes=20 * MIB),
@@ -269,22 +314,16 @@
     zero_rows, zero_width = zero_weight.shape[1:]
     one_rows, parts, one_width = one_weight.shape[1:]
     harmonics = wigner_rows.shape[2]
-    packed = jnp.concatenate(
-        [
-            lane_tiles(zero_weight[0]),
-            lane_tiles(one_weight[0].transpose(1, 0, 2).reshape(parts * one_rows, one_width)),
-        ],
-        axis=0,
-    )
-    chunks = copies_from_all(packed, "z")
+    copies = spread(zero_weight[0], one_weight[0], lax.axis_size("z"))
+    chunks = lax.all_to_all(copies, "z", 0, 0, tiled=True)
     mine = node_features[0].reshape(-1, LANES)
     line = [mine]
     for k in range(1, ys):
         line.append(turned(mine, "yl", -k))
     line = jnp.concatenate(line, axis=0)
-    plane = [line]
-    for k in range(1, xs):
-        plane.append(turned(line, "x", -k))
+    plane = [line] * xs
+    for k in FAR_FIRST:
+        plane[k] = turned(line, "x", -k)
 
     edge_gate = envelope[0] * pad_mask[0].astype(jnp.float32)
     padding = ((0, 0), (0, PAD - harmonics), (0, 0))
@@ -309,16 +348,15 @@
     swapped = turned(send, "c", 1)
     outgoing = added(other, swapped[1])
     arrived = turned(outgoing, "yh", 1)
-    pieces = [p.reshape(-1, harmonics, LANES) for p in plane]
-    arrived, pieces = lax.optimization_barrier((arrived, pieces))
+    pieces = [p.reshape(-1, harmonics, 8, LANES) for p in plane]
     merged = added(added(own, swapped[0]), arrived)
     column = [merged]
     for k in range(1, ys):
         column.append(turned(merged, "yl", -k))
     column = jnp.stack(column)
-    columns = [column]
-    for k in range(1, xs):
-        columns.append(turned(column, "x", -k))
+    columns = [column] * xs
+    for k in FAR_FIRST:
+        columns[k] = turned(column, "x", -k)
     rotated = rotate(slots, edges_from, pieces, wigner)
     update = convolve(
         there,

time: 141 us -> 127 us (0.901)
  local copies, waits for them, and re-layouts: 14.9 us -> 2.97 us
  waiting for transfers between devices: 52 us -> 44.8 us
  starting transfers between devices: 54.3 us -> 60.6 us
  other arithmetic: 3.07 us -> 0.56 us
    ppermute x14, waiting for transfers between devices: 28.2 us -> 19.7 us  [turned(): lax.ppermute(value, axis, [(i, (i + by) % size) for i in range(size)])]
    ppermute x14, starting transfers between devices: 44.1 us -> 49.7 us  [turned(): lax.ppermute(value, axis, [(i, (i + by) % size) for i in range(size)])]
    reshape x4 -> x0, local copies, waits for them, and re-layouts: 5.37 us -> none  [shards(): pieces = [p.reshape(-1, harmonics, LANES) for p in plane]]
    unnamed x24 -> x23, local copies, waits for them, and re-layouts: 6.35 us -> 2.39 us
    convert_element_type x2, other arithmetic: 1.78 us -> 0.09 us  [added(): return (a.astype(jnp.float32) + b.astype(jnp.float32)).astype(jnp.bfloat16)]
    concatenate x1, local copies, waits for them, and re-layouts: 1.54 us -> 0.02 us  [shards(): line = jnp.concatenate(line, axis=0)]
    pallas_call x0 -> x1, Pallas kernels: none -> 1.42 us  [spread(): pl.pallas_call(spread_kernel, out_shape=jax.ShapeDtypeStruct((copies, til...]
  transfers between devices with their start and end apart: 15 -> 15, of which waited for: 6 -> 3; matrix products, arithmetic and copies ran while one was open for 10% -> 1% of each run, Pallas kernels for 7% -> 6%
where the time goes in v2:
time: 127 us; the launch traced here: 126 us
  starting transfers between devices  60.6 us (48%)
  waiting for transfers between devices  44.8 us (35%)
  Pallas kernels  16.8 us (13%)
  local copies, waits for them, and re-layouts  2.97 us (2%)
    ppermute x14, starting transfers between devices, turned(): lax.ppermute(value, axis, [(i, (i + by) % size) for i in range(size)])  49.7 us
    all_to_all x1, waiting for transfers between devices, shards(): chunks = lax.all_to_all(copies, 'z', 0, 0, tiled=True)  25.1 us
    ppermute x14, waiting for transfers between devices, turned(): lax.ppermute(value, axis, [(i, (i + by) % size) for i in range(size)])  19.7 us
    all_to_all x1, starting transfers between devices, shards(): chunks = lax.all_to_all(copies, 'z', 0, 0, tiled=True)  10.9 us
    pallas_call x1, Pallas kernels, rotate(): pl.pallas_call(rotate_kernel, out_shape=jax.ShapeDtypeStruct((edges, fram...  8.07 us
    pallas_call x1, Pallas kernels, convolve(): pl.pallas_call(lambda *refs: convolve_kernel(zero_shape, one_shape, *refs...  6.2 us
  transfers between devices with their start and end apart: 15, of which 3 were waited for; matrix products, arithmetic and copies ran while one was open for 1% of the time, Pallas kernels for 6%

profile of v2, /device:TPU:1, one launch (start us, length us, event | category | flops | bytes accessed | tf_op | source)
XLA Modules:
  0.0 126.2 jit_solution(15245143786135403861)
XLA Ops:
  0.0 0.0 copy-start
  0.0 0.8 copy-done
  0.8 0.0 copy-start.1
  0.8 0.8 copy-done.1
  1.6 0.0 copy-start.4
  1.6 0.0 copy-start.2
  1.6 1.4 %spread_weights.1 = bf16[8,57,8,128]{3,2,1,0:T(8,128)(2,1)} custom-call(bf16[40,640]{1,0:T(8,128)(2,1)S(1)} %bitcast.57, bf16[32,2,512]{2,1,0:T(2,128)(2,1)S(1)} %bitcast.56), custom_call_target="tpu_custom_call" | custom-call | tf_op jit(solution)/shard_map/spread_weights/pallas_call | solution.py:57
  3.1 0.0 copy-start.6
  3.1 0.0 copy-start.7
  3.1 10.9 %all-to-all-start = ((bf16[8,456,128]{2,1,0:T(8,128)(2,1)}), bf16[8,456,128]{2,1,0:T(8,128)(2,1)S(1)}, u32[]{:S(2)}, u32[]{:S(2)}) async-start(bf16[8,456,128]{2,1,0:T(8,128)(2,1)} %bitcast.4), calls=%async_computation | async-start | bytes 1867776 | tf_op jit(solution)/shard_map/all_to_all | solution.py:318
  14.0 0.0 copy-done.4
  14.0 0.2 reshape.71
  14.1 0.2 dynamic-slice_reduce_fusion
  14.3 0.0 copy-done.2
  14.3 0.2 copy.19
  14.5 0.0 copy-done.6
  14.5 0.0 copy-done.7
  14.6 0.2 multiply_convert_fusion
  14.8 0.0 copy-start.5
  14.8 0.0 copy-start.8
  14.8 0.1 pad.8.refs_6_
  14.9 0.0 copy-start.3
  14.9 0.1 pad.7.refs_4_
  15.0 0.5 copy-done.5
  15.5 0.1 pad_add_fusion.refs_0_
  15.5 0.0 copy-done.8
  15.6 25.1 %all-to-all-done = bf16[8,456,128]{2,1,0:T(8,128)(2,1)S(1)} async-done(((bf16[8,456,128]{2,1,0:T(8,128)(2,1)}), bf16[8,456,128]{2,1,0:T(8,128)(2,1)S(1)}, u32[]{:S(2)}, u32[]{:S(2)}) %all-to-all-start) | async-done | bytes 933920 | tf_op jit(solution)/shard_map/all_to_all | solution.py:318
  40.7 1.1 merge_experts.1
  41.8 2.4 %collective-permute-start = (bf16[2,456,128]{2,1,0:T(8,128)(2,1)S(1)}, bf16[2,456,128]{2,1,0:T(8,128)(2,1)S(1)}, u32[]{:S(2)}, u32[]{:S(2)}) collective-permute-start(bf16[2,456,128]{2,1,0:T(8,128)(2,1)S(1)} %bitcast.59), channel_id=1, source_target_pairs={{0,16},{16,0},{1,17},{17,1},{2,18},{18,2},{3,19},{19,3},{4,20},{20... | collective-permute-start | bytes 700424 | tf_op jit(solution)/shard_map/ppermute | solution.py:25
  44.2 0.0 copy-done.3
  44.3 5.2 %collective-permute-start.8 = (bf16[400,128]{1,0:T(8,128)(2,1)S(1)}, bf16[400,128]{1,0:T(8,128)(2,1)S(1)}, u32[]{:S(2)}, u32[]{:S(2)}) collective-permute-start(bf16[400,128]{1,0:T(8,128)(2,1)S(1)} %reshape_squeeze.3), channel_id=1, source_target_pairs={{0,12},{4,0},{8,4},{12,8},{1,13},{5,1},{9,5},{13,9},{2,14},{6,2},{... | collective-permute-start | bytes 307208 | tf_op jit(solution)/shard_map/ppermute | solution.py:25
  49.6 1.9 %collective-permute-start.9 = (bf16[400,128]{1,0:T(8,128)(2,1)S(1)}, bf16[400,128]{1,0:T(8,128)(2,1)S(1)}, u32[]{:S(2)}, u32[]{:S(2)}) collective-permute-start(bf16[400,128]{1,0:T(8,128)(2,1)S(1)} %reshape_squeeze.3), channel_id=1, source_target_pairs={{0,8},{4,12},{8,0},{12,4},{1,9},{5,13},{9,1},{13,5},{2,10},{6,14},... | collective-permute-start | bytes 307208 | tf_op jit(solution)/shard_map/ppermute | solution.py:25
  51.5 2.3 %collective-permute-start.10 = (bf16[400,128]{1,0:T(8,128)(2,1)S(1)}, bf16[400,128]{1,0:T(8,128)(2,1)S(1)}, u32[]{:S(2)}, u32[]{:S(2)}) collective-permute-start(bf16[400,128]{1,0:T(8,128)(2,1)S(1)} %reshape_squeeze.3), channel_id=1, source_target_pairs={{0,4},{4,8},{8,12},{12,0},{1,5},{5,9},{9,13},{13,1},{2,6},{6,10},{... | collective-permute-start | bytes 307208 | tf_op jit(solution)/shard_map/ppermute | solution.py:25
  53.9 0.0 collective-permute-done.8
  53.9 0.0 collective-permute-done
  54.0 5.7 %collective-permute-start.1 = (bf16[456,128]{1,0:T(8,128)(2,1)S(1)}, bf16[456,128]{1,0:T(8,128)(2,1)S(1)}, u32[]{:S(2)}, u32[]{:S(2)}) collective-permute-start(bf16[456,128]{1,0:T(8,128)(2,1)S(1)} %fusion), channel_id=1, source_target_pairs={{0,256},{256,0},{1,257},{257,1},{2,258},{258,2},{3,259},{259,3},{4... | collective-permute-start | bytes 350216 | tf_op jit(solution)/shard_map/ppermute | solution.py:25
  59.6 0.0 collective-permute-done.9
  59.7 0.0 collective-permute-done.10
  59.7 4.4 %collective-permute-start.11 = (bf16[1600,128]{1,0:T(8,128)(2,1)S(1)}, bf16[1600,128]{1,0:T(8,128)(2,1)S(1)}, u32[]{:S(2)}, u32[]{:S(2)}) collective-permute-start(bf16[1600,128]{1,0:T(8,128)(2,1)S(1)} %constant_dynamic-update-slice_fusion), channel_id=1, source_target_pairs={{0,3},{1,0},{2,1},{3,2},{4,7},{5,4},{6,5},{7,6},{8,11},{9,8},{10,9... | collective-permute-start | bytes 1228808 | tf_op jit(solution)/shard_map/ppermute | solution.py:25
  64.1 0.0 collective-permute-done.1
  64.1 0.1 add_convert_fusion
  64.2 4.8 %collective-permute-start.2 = (bf16[456,128]{1,0:T(8,128)(2,1)S(1)}, bf16[456,128]{1,0:T(8,128)(2,1)S(1)}, u32[]{:S(2)}, u32[]{:S(2)}) collective-permute-start(bf16[456,128]{1,0:T(8,128)(2,1)S(1)} %add_convert_fusion), channel_id=1, source_target_pairs={{0,12},{4,0},{8,4},{12,8},{1,13},{5,1},{9,5},{13,9},{2,14},{6,2},{... | collective-permute-start | bytes 350216 | tf_op jit(solution)/shard_map/ppermute | solution.py:25
  68.9 4.6 %collective-permute-start.3 = (bf16[456,128]{1,0:T(8,128)(2,1)S(1)}, bf16[456,128]{1,0:T(8,128)(2,1)S(1)}, u32[]{:S(2)}, u32[]{:S(2)}) collective-permute-start(bf16[456,128]{1,0:T(8,128)(2,1)S(1)} %add_convert_fusion), channel_id=1, source_target_pairs={{0,8},{4,12},{8,0},{12,4},{1,9},{5,13},{9,1},{13,5},{2,10},{6,14},... | collective-permute-start | bytes 350216 | tf_op jit(solution)/shard_map/ppermute | solution.py:25
  73.5 2.9 %collective-permute-start.4 = (bf16[456,128]{1,0:T(8,128)(2,1)S(1)}, bf16[456,128]{1,0:T(8,128)(2,1)S(1)}, u32[]{:S(2)}, u32[]{:S(2)}) collective-permute-start(bf16[456,128]{1,0:T(8,128)(2,1)S(1)} %add_convert_fusion), channel_id=1, source_target_pairs={{0,4},{4,8},{8,12},{12,0},{1,5},{5,9},{9,13},{13,1},{2,6},{6,10},{... | collective-permute-start | bytes 350216 | tf_op jit(solution)/shard_map/ppermute | solution.py:25
  76.4 4.7 %collective-permute-start.12 = (bf16[1600,128]{1,0:T(8,128)(2,1)S(1)}, bf16[1600,128]{1,0:T(8,128)(2,1)S(1)}, u32[]{:S(2)}, u32[]{:S(2)}) collective-permute-start(bf16[1600,128]{1,0:T(8,128)(2,1)S(1)} %constant_dynamic-update-slice_fusion), channel_id=1, source_target_pairs={{0,2},{1,3},{2,0},{3,1},{4,6},{5,7},{6,4},{7,5},{8,10},{9,11},{10,... | collective-permute-start | bytes 1228808 | tf_op jit(solution)/shard_map/ppermute | solution.py:25
  81.1 0.0 collective-permute-done.2
  81.1 2.2 %collective-permute-start.13 = (bf16[1600,128]{1,0:T(8,128)(2,1)S(1)}, bf16[1600,128]{1,0:T(8,128)(2,1)S(1)}, u32[]{:S(2)}, u32[]{:S(2)}) collective-permute-start(bf16[1600,128]{1,0:T(8,128)(2,1)S(1)} %constant_dynamic-update-slice_fusion), channel_id=1, source_target_pairs={{0,1},{1,2},{2,3},{3,0},{4,5},{5,6},{6,7},{7,4},{8,9},{9,10},{10,1... | collective-permute-start | bytes 1228808 | tf_op jit(solution)/shard_map/ppermute | solution.py:25
  83.3 0.0 collective-permute-done.3
  83.3 0.0 collective-permute-done.4
  83.3 0.1 pad_maximum_fusion.1
  83.4 4.3 %collective-permute-start.5 = (bf16[4,456,128]{2,1,0:T(8,128)(2,1)S(1)}, bf16[4,456,128]{2,1,0:T(8,128)(2,1)S(1)}, u32[]{:S(2)}, u32[]{:S(2)}) collective-permute-start(bf16[4,456,128]{2,1,0:T(8,128)(2,1)S(1)} %pad_maximum_fusion.1), channel_id=1, source_target_pairs={{0,3},{1,0},{2,1},{3,2},{4,7},{5,4},{6,5},{7,6},{8,11},{9,8},{10,9... | collective-permute-start | bytes 1400840 | tf_op jit(solution)/shard_map/ppermute | solution.py:25
  87.7 1.9 %collective-permute-start.6 = (bf16[4,456,128]{2,1,0:T(8,128)(2,1)S(1)}, bf16[4,456,128]{2,1,0:T(8,128)(2,1)S(1)}, u32[]{:S(2)}, u32[]{:S(2)}) collective-permute-start(bf16[4,456,128]{2,1,0:T(8,128)(2,1)S(1)} %pad_maximum_fusion.1), channel_id=1, source_target_pairs={{0,2},{1,3},{2,0},{3,1},{4,6},{5,7},{6,4},{7,5},{8,10},{9,11},{10,... | collective-permute-start | bytes 1400840 | tf_op jit(solution)/shard_map/ppermute | solution.py:25
  89.6 0.0 collective-permute-done.11
  89.6 2.5 %collective-permute-start.7 = (bf16[4,456,128]{2,1,0:T(8,128)(2,1)S(1)}, bf16[4,456,128]{2,1,0:T(8,128)(2,1)S(1)}, u32[]{:S(2)}, u32[]{:S(2)}) collective-permute-start(bf16[4,456,128]{2,1,0:T(8,128)(2,1)S(1)} %pad_maximum_fusion.1), channel_id=1, source_target_pairs={{0,1},{1,2},{2,3},{3,0},{4,5},{5,6},{6,7},{7,4},{8,9},{9,10},{10,1... | collective-permute-start | bytes 1400840 | tf_op jit(solution)/shard_map/ppermute | solution.py:25
  92.1 0.0 collective-permute-done.12
  92.1 9.7 %collective-permute-done.13 = bf16[1600,128]{1,0:T(8,128)(2,1)S(1)} collective-permute-done((bf16[1600,128]{1,0:T(8,128)(2,1)S(1)}, bf16[1600,128]{1,0:T(8,128)(2,1)S(1)}, u32[]{:S(2)}, u32[]{:S(2)}) %collective-permute-start.13) | collective-permute-done | bytes 409632 | tf_op jit(solution)/shard_map/ppermute | solution.py:25
  101.8 8.1 %rotate_edges.1.refs_5_ = bf16[1152,1664]{1,0:T(8,128)(2,1)S(1)} custom-call(s32[256]{0:T(256)S(1)} %fusion.4.slot_ref, s32[1152]{0:T(1024)S(1)} %reduce.1.neighbour_ref, bf16[8,25,8,128]{3,2,1,0:T(8,128)(2,1)S(1)} %bitcast.49, bf16[8,25,8,128]{3,2,1,0:T(8,128)(2,1)S(1)} %bitcast.53, bf16[8,25,8,128]{3,2,1,0:T(8,128)(2,1)S(1)} %bitcast.54, ...), custom_call_target="tpu_custom_call" | custom-call | tf_op jit(solution)/shard_map/rotate_edges/pallas_call | solution.py:174
  109.9 0.1 pad_maximum_fusion.refs_1_
  109.9 0.0 collective-permute-done.5
  109.9 0.0 collective-permute-done.6
  109.9 10.0 %collective-permute-done.7 = bf16[4,456,128]{2,1,0:T(8,128)(2,1)S(1)} collective-permute-done((bf16[4,456,128]{2,1,0:T(8,128)(2,1)S(1)}, bf16[4,456,128]{2,1,0:T(8,128)(2,1)S(1)}, u32[]{:S(2)}, u32[]{:S(2)}) %collective-permute-start.7) | collective-permute-done | bytes 466976 | tf_op jit(solution)/shard_map/ppermute | solution.py:25
  120.0 6.2 %convolve_edges.1 = bf16[25,16,128]{2,1,0:T(8,128)(2,1)} custom-call(s32[2]{0:T(128)S(1)} %pad_add_fusion.refs_0_, bf16[4,57,8,128]{3,2,1,0:T(8,128)(2,1)S(1)} %pad_maximum_fusion.refs_1_, bf16[4,57,8,128]{3,2,1,0:T(8,128)(2,1)S(1)} %bitcast.50, bf16[4,57,8,128]{3,2,1,0:T(8,128)(2,1)S(1)} %bitcast.51, bf16[4,57,8,128]{3,2,1,0:T(8,128)(2,1)S(1)} %bitcast.52, ...), custom_call_target="tpu_custom_call" | custom-call | tf_op jit(solution)/shard_map/convolve_edges/pallas_call | solution.py:276
  (13 shorter events, 0.3 us)
Async XLA Ops:
  0.0 0.8 copy-start
  0.8 0.8 copy-start.1
  1.6 12.3 %copy-start.4 = (f32[32,32]{1,0:T(8,128)S(1)}, f32[32,32]{1,0:T(8,128)}, u32[]{:S(2)}) copy-start(f32[32,32]{1,0:T(8,128)} %param.15) | copy-start | bytes 12292
  1.6 12.7 %copy-start.2 = (bf16[1,13,25,1152]{3,1,2,0:T(8,128)(2,1)S(1)}, bf16[1,13,25,1152]{3,1,2,0:T(8,128)(2,1)}, u32[]{:S(2)}) copy-start(bf16[1,13,25,1152]{3,1,2,0:T(8,128)(2,1)} %param.14) | copy-start | bytes 2246404
  3.1 11.4 %copy-start.6 = (f32[1,1152]{1,0:T(1,128)S(1)}, f32[1,1152]{1,0:T(1,128)}, u32[]{:S(2)}) copy-start(f32[1,1152]{1,0:T(1,128)} %param.13) | copy-start | bytes 13828
  3.1 11.4 %copy-start.7 = (s32[1,1152]{1,0:T(1,128)S(1)}, s32[1,1152]{1,0:T(1,128)}, u32[]{:S(2)}) copy-start(s32[1,1152]{1,0:T(1,128)} %param.12) | copy-start | bytes 13828
  3.1 37.6 %all-to-all-start = ((bf16[8,456,128]{2,1,0:T(8,128)(2,1)}), bf16[8,456,128]{2,1,0:T(8,128)(2,1)S(1)}, u32[]{:S(2)}, u32[]{:S(2)}) async-start(bf16[8,456,128]{2,1,0:T(8,128)(2,1)} %bitcast.4), calls=%async_computation | async-start | bytes 1867776 | tf_op jit(solution)/shard_map/all_to_all | solution.py:318
  14.8 0.7 copy-start.5
  14.8 0.8 copy-start.8
  14.9 29.4 %copy-start.3 = (bf16[1,16,25,128]{3,1,2,0:T(8,128)(2,1)S(1)}, bf16[1,16,25,128]{3,1,2,0:T(8,128)(2,1)}, u32[]{:S(2)}) copy-start(bf16[1,16,25,128]{3,1,2,0:T(8,128)(2,1)} %param.9) | copy-start | bytes 307204
  41.8 12.1 %collective-permute-start = (bf16[2,456,128]{2,1,0:T(8,128)(2,1)S(1)}, bf16[2,456,128]{2,1,0:T(8,128)(2,1)S(1)}, u32[]{:S(2)}, u32[]{:S(2)}) collective-permute-start(bf16[2,456,128]{2,1,0:T(8,128)(2,1)S(1)} %bitcast.59), channel_id=1, source_target_pairs={{0,16},{16,0},{1,17},{17,1},{2,18},{18,2},{3,19},{19,3},{4,20},{20... | collective-permute-start | bytes 700424 | tf_op jit(solution)/shard_map/ppermute | solution.py:25
  44.3 9.5 %collective-permute-start.8 = (bf16[400,128]{1,0:T(8,128)(2,1)S(1)}, bf16[400,128]{1,0:T(8,128)(2,1)S(1)}, u32[]{:S(2)}, u32[]{:S(2)}) collective-permute-start(bf16[400,128]{1,0:T(8,128)(2,1)S(1)} %reshape_squeeze.3), channel_id=1, source_target_pairs={{0,12},{4,0},{8,4},{12,8},{1,13},{5,1},{9,5},{13,9},{2,14},{6,2},{... | collective-permute-start | bytes 307208 | tf_op jit(solution)/shard_map/ppermute | solution.py:25
  49.6 10.1 %collective-permute-start.9 = (bf16[400,128]{1,0:T(8,128)(2,1)S(1)}, bf16[400,128]{1,0:T(8,128)(2,1)S(1)}, u32[]{:S(2)}, u32[]{:S(2)}) collective-permute-start(bf16[400,128]{1,0:T(8,128)(2,1)S(1)} %reshape_squeeze.3), channel_id=1, source_target_pairs={{0,8},{4,12},{8,0},{12,4},{1,9},{5,13},{9,1},{13,5},{2,10},{6,14},... | collective-permute-start | bytes 307208 | tf_op jit(solution)/shard_map/ppermute | solution.py:25
  51.5 8.2 %collective-permute-start.10 = (bf16[400,128]{1,0:T(8,128)(2,1)S(1)}, bf16[400,128]{1,0:T(8,128)(2,1)S(1)}, u32[]{:S(2)}, u32[]{:S(2)}) collective-permute-start(bf16[400,128]{1,0:T(8,128)(2,1)S(1)} %reshape_squeeze.3), channel_id=1, source_target_pairs={{0,4},{4,8},{8,12},{12,0},{1,5},{5,9},{9,13},{13,1},{2,6},{6,10},{... | collective-permute-start | bytes 307208 | tf_op jit(solution)/shard_map/ppermute | solution.py:25
  54.0 10.1 %collective-permute-start.1 = (bf16[456,128]{1,0:T(8,128)(2,1)S(1)}, bf16[456,128]{1,0:T(8,128)(2,1)S(1)}, u32[]{:S(2)}, u32[]{:S(2)}) collective-permute-start(bf16[456,128]{1,0:T(8,128)(2,1)S(1)} %fusion), channel_id=1, source_target_pairs={{0,256},{256,0},{1,257},{257,1},{2,258},{258,2},{3,259},{259,3},{4... | collective-permute-start | bytes 350216 | tf_op jit(solution)/shard_map/ppermute | solution.py:25
  59.7 29.9 %collective-permute-start.11 = (bf16[1600,128]{1,0:T(8,128)(2,1)S(1)}, bf16[1600,128]{1,0:T(8,128)(2,1)S(1)}, u32[]{:S(2)}, u32[]{:S(2)}) collective-permute-start(bf16[1600,128]{1,0:T(8,128)(2,1)S(1)} %constant_dynamic-update-slice_fusion), channel_id=1, source_target_pairs={{0,3},{1,0},{2,1},{3,2},{4,7},{5,4},{6,5},{7,6},{8,11},{9,8},{10,9... | collective-permute-start | bytes 1228808 | tf_op jit(solution)/shard_map/ppermute | solution.py:25
  64.2 16.9 %collective-permute-start.2 = (bf16[456,128]{1,0:T(8,128)(2,1)S(1)}, bf16[456,128]{1,0:T(8,128)(2,1)S(1)}, u32[]{:S(2)}, u32[]{:S(2)}) collective-permute-start(bf16[456,128]{1,0:T(8,128)(2,1)S(1)} %add_convert_fusion), channel_id=1, source_target_pairs={{0,12},{4,0},{8,4},{12,8},{1,13},{5,1},{9,5},{13,9},{2,14},{6,2},{... | collective-permute-start | bytes 350216 | tf_op jit(solution)/shard_map/ppermute | solution.py:25
  68.9 14.4 %collective-permute-start.3 = (bf16[456,128]{1,0:T(8,128)(2,1)S(1)}, bf16[456,128]{1,0:T(8,128)(2,1)S(1)}, u32[]{:S(2)}, u32[]{:S(2)}) collective-permute-start(bf16[456,128]{1,0:T(8,128)(2,1)S(1)} %add_convert_fusion), channel_id=1, source_target_pairs={{0,8},{4,12},{8,0},{12,4},{1,9},{5,13},{9,1},{13,5},{2,10},{6,14},... | collective-permute-start | bytes 350216 | tf_op jit(solution)/shard_map/ppermute | solution.py:25
  73.5 9.8 %collective-permute-start.4 = (bf16[456,128]{1,0:T(8,128)(2,1)S(1)}, bf16[456,128]{1,0:T(8,128)(2,1)S(1)}, u32[]{:S(2)}, u32[]{:S(2)}) collective-permute-start(bf16[456,128]{1,0:T(8,128)(2,1)S(1)} %add_convert_fusion), channel_id=1, source_target_pairs={{0,4},{4,8},{8,12},{12,0},{1,5},{5,9},{9,13},{13,1},{2,6},{6,10},{... | collective-permute-start | bytes 350216 | tf_op jit(solution)/shard_map/ppermute | solution.py:25
  76.4 15.7 %collective-permute-start.12 = (bf16[1600,128]{1,0:T(8,128)(2,1)S(1)}, bf16[1600,128]{1,0:T(8,128)(2,1)S(1)}, u32[]{:S(2)}, u32[]{:S(2)}) collective-permute-start(bf16[1600,128]{1,0:T(8,128)(2,1)S(1)} %constant_dynamic-update-slice_fusion), channel_id=1, source_target_pairs={{0,2},{1,3},{2,0},{3,1},{4,6},{5,7},{6,4},{7,5},{8,10},{9,11},{10,... | collective-permute-start | bytes 1228808 | tf_op jit(solution)/shard_map/ppermute | solution.py:25
  81.1 20.7 %collective-permute-start.13 = (bf16[1600,128]{1,0:T(8,128)(2,1)S(1)}, bf16[1600,128]{1,0:T(8,128)(2,1)S(1)}, u32[]{:S(2)}, u32[]{:S(2)}) collective-permute-start(bf16[1600,128]{1,0:T(8,128)(2,1)S(1)} %constant_dynamic-update-slice_fusion), channel_id=1, source_target_pairs={{0,1},{1,2},{2,3},{3,0},{4,5},{5,6},{6,7},{7,4},{8,9},{9,10},{10,1... | collective-permute-start | bytes 1228808 | tf_op jit(solution)/shard_map/ppermute | solution.py:25
  83.4 26.5 %collective-permute-start.5 = (bf16[4,456,128]{2,1,0:T(8,128)(2,1)S(1)}, bf16[4,456,128]{2,1,0:T(8,128)(2,1)S(1)}, u32[]{:S(2)}, u32[]{:S(2)}) collective-permute-start(bf16[4,456,128]{2,1,0:T(8,128)(2,1)S(1)} %pad_maximum_fusion.1), channel_id=1, source_target_pairs={{0,3},{1,0},{2,1},{3,2},{4,7},{5,4},{6,5},{7,6},{8,11},{9,8},{10,9... | collective-permute-start | bytes 1400840 | tf_op jit(solution)/shard_map/ppermute | solution.py:25
  87.7 22.3 %collective-permute-start.6 = (bf16[4,456,128]{2,1,0:T(8,128)(2,1)S(1)}, bf16[4,456,128]{2,1,0:T(8,128)(2,1)S(1)}, u32[]{:S(2)}, u32[]{:S(2)}) collective-permute-start(bf16[4,456,128]{2,1,0:T(8,128)(2,1)S(1)} %pad_maximum_fusion.1), channel_id=1, source_target_pairs={{0,2},{1,3},{2,0},{3,1},{4,6},{5,7},{6,4},{7,5},{8,10},{9,11},{10,... | collective-permute-start | bytes 1400840 | tf_op jit(solution)/shard_map/ppermute | solution.py:25
  89.6 30.4 %collective-permute-start.7 = (bf16[4,456,128]{2,1,0:T(8,128)(2,1)S(1)}, bf16[4,456,128]{2,1,0:T(8,128)(2,1)S(1)}, u32[]{:S(2)}, u32[]{:S(2)}) collective-permute-start(bf16[4,456,128]{2,1,0:T(8,128)(2,1)S(1)} %pad_maximum_fusion.1), channel_id=1, source_target_pairs={{0,1},{1,2},{2,3},{3,0},{4,5},{5,6},{6,7},{7,4},{8,9},{9,10},{10,1... | collective-permute-start | bytes 1400840 | tf_op jit(solution)/shard_map/ppermute | solution.py:25

commit v3 on v2

--- a/solution.py
+++ b/solution.py
@@ -64,7 +64,6 @@
             pltpu.VMEM(one.shape, one.dtype),
             pltpu.SemaphoreType.DMA((2,)),
         ],
-        compiler_params=pltpu.CompilerParams(vmem_limit_bytes=8 * MIB),
         name="spread_weights",
     )(zero, one)
     return out.reshape(copies, tiles * 8, LANES)
@@ -104,10 +103,32 @@
     return tuple(o.reshape(-1, rows, lanes) if o.ndim == 4 else o.reshape(rows, lanes) for o in outs)
 
 
+def atoms_of(block):
+    return block * LANES // NEIGH, ((block + 1) * LANES - 1) // NEIGH + 1
+
+
+def pick_atoms(gated_ref, picked_ref):
+    lane = lax.broadcasted_iota(jnp.int32, (PAD, LANES), 1)
+    for b in range(picked_ref.shape[0]):
+        low = b * LANES
+        first, last = atoms_of(b)
+        for r in range(gated_ref.shape[0]):
+            w = gated_ref[r, :, low : low + LANES]
+            for a in range(first, last):
+                inside = (lane + low >= a * NEIGH) & (lane + low < (a + 1) * NEIGH)
+                picked_ref[
+                    b,
+                    r // 2,
+                    (a - first) * PAD : (a - first + 1) * PAD,
+                    r % 2 * LANES : (r % 2 + 1) * LANES,
+                ] = jnp.where(inside, w, jnp.zeros_like(w))
+
+
 def rotate_kernel(slot_ref, neighbour_ref, *refs):
     piece_refs = refs[:4]
-    wigner_ref, out_ref, feature_ref, row_ref, spread_ref = refs[4:]
+    wigner_ref, gated_ref, out_ref, picked_ref, feature_ref, row_ref, spread_ref = refs[4:]
     frame = wigner_ref.shape[0]
+    pick_atoms(gated_ref, picked_ref)
     runs, harmonics = piece_refs[0].shape[:2]
     row_ref[:, 8 * harmonics :] = jnp.zeros_like(row_ref[:, 8 * harmonics :])
 
@@ -156,44 +177,51 @@
                         rows, stacked, (((1,), (0,)), ((), ())), preferred_element_type=jnp.float32
                     )
                 )
+            rows = pl.ds(pl.multiple_of(start + 2 * GROUP * pair, 2 * GROUP), 2 * GROUP)
+            both = []
             for r in range(frame):
-                both = jnp.concatenate([h[GROUP * r : GROUP * (r + 1)] for h in halves], axis=0)
-                out_ref[
-                    pl.ds(pl.multiple_of(start + 2 * GROUP * pair, 2 * GROUP), 2 * GROUP),
-                    r * LANES : (r + 1) * LANES,
-                ] = both.astype(out_ref.dtype)
+                tile = jnp.concatenate([h[GROUP * r : GROUP * (r + 1)] for h in halves], axis=0)
+                tile = tile.astype(out_ref.dtype)
+                out_ref[rows, r * LANES : (r + 1) * LANES] = tile
+                both.append(tile.astype(jnp.float32))
+            for m in range(LMAX):
+                tile = both[LMAX + 1 + m] + both[2 * LMAX + 1 + m]
+                out_ref[rows, (frame + m) * LANES : (frame + m + 1) * LANES] = tile.astype(out_ref.dtype)
         return carry
 
     lax.fori_loop(0, neighbour_ref.shape[0] // block, one_block, 0)
 
 
-def rotate(slots, neighbour, pieces, wigner):
+def rotate(slots, neighbour, pieces, wigner, gated):
     frame, _, edges = wigner.shape
     runs, harmonics = pieces[0].shape[:2]
     atoms = len(pieces) * runs * 8
     return pl.pallas_call(
         rotate_kernel,
-        out_shape=jax.ShapeDtypeStruct((edges, frame * LANES), jnp.bfloat16),
+        out_shape=(
+            jax.ShapeDtypeStruct((edges, (frame + LMAX) * LANES), jnp.bfloat16),
+            jax.ShapeDtypeStruct((edges // LANES, (frame + 1) // 2, 3 * PAD, 2 * LANES), jnp.bfloat16),
+        ),
         in_specs=[
             pl.BlockSpec(memory_space=pltpu.SMEM),
             pl.BlockSpec(memory_space=pltpu.SMEM),
         ]
-        + [pl.BlockSpec(memory_space=pltpu.VMEM)] * (len(pieces) + 1),
-        out_specs=pl.BlockSpec(memory_space=pltpu.VMEM),
+        + [pl.BlockSpec(memory_space=pltpu.VMEM)] * (len(pieces) + 2),
+        out_specs=(pl.BlockSpec(memory_space=pltpu.VMEM), pl.BlockSpec(memory_space=pltpu.VMEM)),
         scratch_shapes=[
             pltpu.VMEM((atoms, PAD, LANES), jnp.bfloat16),
             pltpu.VMEM((len(pieces), 8 * harmonics + 8, LANES), jnp.float32),
             pltpu.VMEM((frame, LANES, GROUP * PAD), jnp.float32),
         ],
-        compiler_params=pltpu.CompilerParams(vmem_limit_bytes=20 * MIB),
+        compiler_params=pltpu.CompilerParams(vmem_limit_bytes=26 * MIB),
         name="rotate_edges",
-    )(slots, neighbour, *pieces, wigner)
+    )(slots, neighbour, *pieces, wigner, gated)
 
 
 def convolve_kernel(zero_shape, one_shape, x_ref, *refs):
     xs = 4
     column_refs = refs[:xs]
-    rotated_ref, wigner_ref, out_ref, zero32, one32, zero16, real16, imag16, message, total = refs[xs:]
+    rotated_ref, picked_ref, out_ref, zero32, one32, zero16, real16, sum16, diff16, message, total = refs[xs:]
     zero_rows, zero_width = zero_shape
     parts, one_rows, one_width = one_shape
     ys = column_refs[0].shape[0]
@@ -218,10 +246,11 @@
                         ].astype(jnp.float32)
     zero16[...] = zero32[...].astype(jnp.bfloat16)
     real16[...] = one32[0].astype(jnp.bfloat16)
-    imag16[...] = one32[1].astype(jnp.bfloat16)
+    sum16[...] = (one32[0] + one32[1]).astype(jnp.bfloat16)
+    diff16[...] = (one32[1] - one32[0]).astype(jnp.bfloat16)
 
     edges = rotated_ref.shape[0]
-    frame = wigner_ref.shape[0]
+    frame = 3 * LMAX + 1
     atoms = edges // NEIGH
     side = LMAX * LANES
     near = zero_width
@@ -234,41 +263,32 @@
         span = slice(b * rows, (b + 1) * rows)
         message[span, :near] = times(rotated_ref[span, :near], zero16).astype(jnp.bfloat16)
         plus = rotated_ref[span, near : near + side]
-        minus = rotated_ref[span, near + side :]
-        message[span, near : near + side] = (times(plus, real16) - times(minus, imag16)).astype(jnp.bfloat16)
-        message[span, near + side :] = (times(plus, imag16) + times(minus, real16)).astype(jnp.bfloat16)
+        minus = rotated_ref[span, near + side : near + 2 * side]
+        shared = times(rotated_ref[span, near + 2 * side :], real16)
+        message[span, near : near + side] = (shared - times(minus, sum16)).astype(jnp.bfloat16)
+        message[span, near + side :] = (shared + times(plus, diff16)).astype(jnp.bfloat16)
 
     total[...] = jnp.zeros_like(total)
-    lane = lax.broadcasted_iota(jnp.int32, (PAD, LANES), 1)
     for b in range(edges // LANES):
         low = b * LANES
-        first_atom = low // NEIGH
-        last_atom = (low + LANES - 1) // NEIGH
+        first, last = atoms_of(b)
         part = None
         for r0 in range(0, frame, 2):
             pair = [r for r in (r0, r0 + 1) if r < frame]
-            left = []
-            for r in pair:
-                w = wigner_ref[r, :, low : low + LANES]
-                picks = []
-                for a in range(first_atom, last_atom + 1):
-                    inside = (lane + low >= a * NEIGH) & (lane + low < (a + 1) * NEIGH)
-                    picks.append(jnp.where(inside, w, jnp.zeros_like(w)))
-                left.append(jnp.concatenate(picks, axis=0))
-            lhs = jnp.concatenate(left, axis=1)
+            lhs = picked_ref[b, r0 // 2, : (last - first) * PAD, : len(pair) * LANES]
             rhs = jnp.concatenate(
                 [message[low : low + LANES, r * LANES : (r + 1) * LANES] for r in pair], axis=0
             )
             got = lax.dot_general(lhs, rhs, (((1,), (0,)), ((), ())), preferred_element_type=jnp.float32)
             part = got if part is None else part + got
-        window = slice(first_atom * PAD, (last_atom + 1) * PAD)
+        window = slice(first * PAD, last * PAD)
         total[window, :] = total[window, :] + part
     for k in range(out_ref.shape[0]):
         row = total[pl.ds(k, atoms, stride=PAD), :]
         out_ref[k] = (row * (1.0 / math.sqrt(NEIGH))).astype(out_ref.dtype)
 
 
-def convolve(x, columns, rotated, wigner, zero_shape, one_shape, harmonics):
+def convolve(x, columns, rotated, picked, zero_shape, one_shape, harmonics):
     edges = rotated.shape[0]
     atoms = edges // NEIGH
     parts, _, one_width = one_shape
@@ -285,12 +305,13 @@
             pltpu.VMEM((total_zero, total_zero), jnp.bfloat16),
             pltpu.VMEM((total_one, total_one), jnp.bfloat16),
             pltpu.VMEM((total_one, total_one), jnp.bfloat16),
-            pltpu.VMEM((edges, rotated.shape[1]), jnp.bfloat16),
+            pltpu.VMEM((total_one, total_one), jnp.bfloat16),
+            pltpu.VMEM((edges, total_zero + parts * total_one), jnp.bfloat16),
             pltpu.VMEM((atoms * PAD, LANES), jnp.float32),
         ],
         compiler_params=pltpu.CompilerParams(vmem_limit_bytes=28 * MIB),
         name="convolve_edges",
-    )(x, *columns, rotated, wigner)
+    )(x, *columns, rotated, picked)
 
 
 def added(a, b):
@@ -357,12 +378,12 @@
     columns = [column] * xs
     for k in FAR_FIRST:
         columns[k] = turned(column, "x", -k)
-    rotated = rotate(slots, edges_from, pieces, wigner)
+    rotated, gathered = rotate(slots, edges_from, pieces, wigner, gated)
     update = convolve(
         there,
         [m.reshape(ys, -1, 8, LANES) for m in columns],
         rotated,
-        gated,
+        gathered,
         (zero_rows, zero_width),
         (parts, one_rows, one_width),
         harmonics,

time: 127 us -> 126 us (level)
  local copies, waits for them, and re-layouts: 2.97 us -> 1.32 us
    unnamed x23 -> x19, local copies, waits for them, and re-layouts: 2.39 us -> 0.74 us
  transfers between devices with their start and end apart: 15 -> 15, of which waited for: 3 -> 3; matrix products, arithmetic and copies ran while one was open for 1% -> 1% of each run, Pallas kernels for 6% -> 7%
where the time goes in v3:
time: 126 us; the launch traced here: 125 us
  starting transfers between devices  60.6 us (48%)
  waiting for transfers between devices  44.3 us (35%)
  Pallas kernels  17.7 us (14%)
  local copies, waits for them, and re-layouts  1.32 us (1%)
    ppermute x14, starting transfers between devices, turned(): lax.ppermute(value, axis, [(i, (i + by) % size) for i in range(size)])  49.7 us
    all_to_all x1, waiting for transfers between devices, shards(): chunks = lax.all_to_all(copies, 'z', 0, 0, tiled=True)  25.1 us
    ppermute x14, waiting for transfers between devices, turned(): lax.ppermute(value, axis, [(i, (i + by) % size) for i in range(size)])  19.2 us
    all_to_all x1, starting transfers between devices, shards(): chunks = lax.all_to_all(copies, 'z', 0, 0, tiled=True)  10.9 us
    pallas_call x1, Pallas kernels, rotate(): pl.pallas_call(rotate_kernel, out_shape=(jax.ShapeDtypeStruct((edges, (fr...  8.57 us
    pallas_call x1, Pallas kernels, convolve(): pl.pallas_call(lambda *refs: convolve_kernel(zero_shape, one_shape, *refs...  5.8 us
  transfers between devices with their start and end apart: 15, of which 3 were waited for; matrix products, arithmetic and copies ran while one was open for 1% of the time, Pallas kernels for 7%

profile of v3, /device:TPU:1, one launch (start us, length us, event | category | flops | bytes accessed | tf_op | source)
XLA Modules:
  0.0 124.9 jit_solution(3827618045602549262)
XLA Ops:
  0.0 0.0 copy-start.2
  0.0 0.0 copy-start
  0.0 2.2 %spread_weights.1 = bf16[8,57,8,128]{3,2,1,0:T(8,128)(2,1)} custom-call(bf16[40,640]{1,0:T(8,128)(2,1)} %bitcast.69, bf16[32,2,512]{2,1,0:T(2,128)(2,1)} %bitcast.68), custom_call_target="tpu_custom_call" | custom-call | tf_op jit(solution)/shard_map/spread_weights/pallas_call | solution.py:57
  2.2 0.0 copy-start.4
  2.2 0.0 copy-start.5
  2.2 10.9 %all-to-all-start = ((bf16[8,456,128]{2,1,0:T(8,128)(2,1)}), bf16[8,456,128]{2,1,0:T(8,128)(2,1)S(1)}, u32[]{:S(2)}, u32[]{:S(2)}) async-start(bf16[8,456,128]{2,1,0:T(8,128)(2,1)} %bitcast.59), calls=%async_computation | async-start | bytes 1867776 | tf_op jit(solution)/shard_map/all_to_all | solution.py:339
  13.1 0.0 copy-done.2
  13.1 0.2 reshape.71
  13.3 0.2 dynamic-slice_reduce_fusion
  13.5 0.0 copy-done
  13.5 0.2 copy.19
  13.7 0.0 copy-done.4
  13.7 0.0 copy-done.5
  13.7 0.2 multiply_convert_fusion
  13.9 0.0 copy-start.3
  13.9 0.0 copy-start.6
  13.9 0.1 pad.8.refs_5_
  14.0 0.0 copy-start.1
  14.0 0.1 pad.7.refs_4_
  14.1 0.5 copy-done.3
  14.6 0.1 pad_add_fusion.refs_0_
  14.7 0.0 copy-done.6
  14.7 25.1 %all-to-all-done = bf16[8,456,128]{2,1,0:T(8,128)(2,1)S(1)} async-done(((bf16[8,456,128]{2,1,0:T(8,128)(2,1)}), bf16[8,456,128]{2,1,0:T(8,128)(2,1)S(1)}, u32[]{:S(2)}, u32[]{:S(2)}) %all-to-all-start) | async-done | bytes 933920 | tf_op jit(solution)/shard_map/all_to_all | solution.py:339
  39.8 1.1 merge_experts.1
  41.0 2.4 %collective-permute-start = (bf16[2,456,128]{2,1,0:T(8,128)(2,1)S(1)}, bf16[2,456,128]{2,1,0:T(8,128)(2,1)S(1)}, u32[]{:S(2)}, u32[]{:S(2)}) collective-permute-start(bf16[2,456,128]{2,1,0:T(8,128)(2,1)S(1)} %bitcast.57), channel_id=1, source_target_pairs={{0,16},{16,0},{1,17},{17,1},{2,18},{18,2},{3,19},{19,3},{4,20},{20... | collective-permute-start | bytes 700424 | tf_op jit(solution)/shard_map/ppermute | solution.py:25
  43.4 0.0 copy-done.1
  43.5 5.2 %collective-permute-start.8 = (bf16[400,128]{1,0:T(8,128)(2,1)S(1)}, bf16[400,128]{1,0:T(8,128)(2,1)S(1)}, u32[]{:S(2)}, u32[]{:S(2)}) collective-permute-start(bf16[400,128]{1,0:T(8,128)(2,1)S(1)} %reshape_squeeze.3), channel_id=1, source_target_pairs={{0,12},{4,0},{8,4},{12,8},{1,13},{5,1},{9,5},{13,9},{2,14},{6,2},{... | collective-permute-start | bytes 307208 | tf_op jit(solution)/shard_map/ppermute | solution.py:25
  48.7 1.9 %collective-permute-start.9 = (bf16[400,128]{1,0:T(8,128)(2,1)S(1)}, bf16[400,128]{1,0:T(8,128)(2,1)S(1)}, u32[]{:S(2)}, u32[]{:S(2)}) collective-permute-start(bf16[400,128]{1,0:T(8,128)(2,1)S(1)} %reshape_squeeze.3), channel_id=1, source_target_pairs={{0,8},{4,12},{8,0},{12,4},{1,9},{5,13},{9,1},{13,5},{2,10},{6,14},... | collective-permute-start | bytes 307208 | tf_op jit(solution)/shard_map/ppermute | solution.py:25
  50.7 2.3 %collective-permute-start.10 = (bf16[400,128]{1,0:T(8,128)(2,1)S(1)}, bf16[400,128]{1,0:T(8,128)(2,1)S(1)}, u32[]{:S(2)}, u32[]{:S(2)}) collective-permute-start(bf16[400,128]{1,0:T(8,128)(2,1)S(1)} %reshape_squeeze.3), channel_id=1, source_target_pairs={{0,4},{4,8},{8,12},{12,0},{1,5},{5,9},{9,13},{13,1},{2,6},{6,10},{... | collective-permute-start | bytes 307208 | tf_op jit(solution)/shard_map/ppermute | solution.py:25
  53.0 0.0 collective-permute-done.8
  53.1 0.0 collective-permute-done
  53.1 5.7 %collective-permute-start.1 = (bf16[456,128]{1,0:T(8,128)(2,1)S(1)}, bf16[456,128]{1,0:T(8,128)(2,1)S(1)}, u32[]{:S(2)}, u32[]{:S(2)}) collective-permute-start(bf16[456,128]{1,0:T(8,128)(2,1)S(1)} %fusion), channel_id=1, source_target_pairs={{0,256},{256,0},{1,257},{257,1},{2,258},{258,2},{3,259},{259,3},{4... | collective-permute-start | bytes 350216 | tf_op jit(solution)/shard_map/ppermute | solution.py:25
  58.8 0.0 collective-permute-done.9
  58.8 0.0 collective-permute-done.10
  58.8 4.4 %collective-permute-start.11 = (bf16[1600,128]{1,0:T(8,128)(2,1)S(1)}, bf16[1600,128]{1,0:T(8,128)(2,1)S(1)}, u32[]{:S(2)}, u32[]{:S(2)}) collective-permute-start(bf16[1600,128]{1,0:T(8,128)(2,1)S(1)} %constant_dynamic-update-slice_fusion), channel_id=1, source_target_pairs={{0,3},{1,0},{2,1},{3,2},{4,7},{5,4},{6,5},{7,6},{8,11},{9,8},{10,9... | collective-permute-start | bytes 1228808 | tf_op jit(solution)/shard_map/ppermute | solution.py:25
  63.2 0.0 collective-permute-done.1
  63.2 0.1 add_convert_fusion
  63.3 4.8 %collective-permute-start.2 = (bf16[456,128]{1,0:T(8,128)(2,1)S(1)}, bf16[456,128]{1,0:T(8,128)(2,1)S(1)}, u32[]{:S(2)}, u32[]{:S(2)}) collective-permute-start(bf16[456,128]{1,0:T(8,128)(2,1)S(1)} %add_convert_fusion), channel_id=1, source_target_pairs={{0,12},{4,0},{8,4},{12,8},{1,13},{5,1},{9,5},{13,9},{2,14},{6,2},{... | collective-permute-start | bytes 350216 | tf_op jit(solution)/shard_map/ppermute | solution.py:25
  68.1 4.6 %collective-permute-start.3 = (bf16[456,128]{1,0:T(8,128)(2,1)S(1)}, bf16[456,128]{1,0:T(8,128)(2,1)S(1)}, u32[]{:S(2)}, u32[]{:S(2)}) collective-permute-start(bf16[456,128]{1,0:T(8,128)(2,1)S(1)} %add_convert_fusion), channel_id=1, source_target_pairs={{0,8},{4,12},{8,0},{12,4},{1,9},{5,13},{9,1},{13,5},{2,10},{6,14},... | collective-permute-start | bytes 350216 | tf_op jit(solution)/shard_map/ppermute | solution.py:25
  72.7 2.9 %collective-permute-start.4 = (bf16[456,128]{1,0:T(8,128)(2,1)S(1)}, bf16[456,128]{1,0:T(8,128)(2,1)S(1)}, u32[]{:S(2)}, u32[]{:S(2)}) collective-permute-start(bf16[456,128]{1,0:T(8,128)(2,1)S(1)} %add_convert_fusion), channel_id=1, source_target_pairs={{0,4},{4,8},{8,12},{12,0},{1,5},{5,9},{9,13},{13,1},{2,6},{6,10},{... | collective-permute-start | bytes 350216 | tf_op jit(solution)/shard_map/ppermute | solution.py:25
  75.6 4.7 %collective-permute-start.12 = (bf16[1600,128]{1,0:T(8,128)(2,1)S(1)}, bf16[1600,128]{1,0:T(8,128)(2,1)S(1)}, u32[]{:S(2)}, u32[]{:S(2)}) collective-permute-start(bf16[1600,128]{1,0:T(8,128)(2,1)S(1)} %constant_dynamic-update-slice_fusion), channel_id=1, source_target_pairs={{0,2},{1,3},{2,0},{3,1},{4,6},{5,7},{6,4},{7,5},{8,10},{9,11},{10,... | collective-permute-start | bytes 1228808 | tf_op jit(solution)/shard_map/ppermute | solution.py:25
  80.2 0.0 collective-permute-done.2
  80.2 2.2 %collective-permute-start.13 = (bf16[1600,128]{1,0:T(8,128)(2,1)S(1)}, bf16[1600,128]{1,0:T(8,128)(2,1)S(1)}, u32[]{:S(2)}, u32[]{:S(2)}) collective-permute-start(bf16[1600,128]{1,0:T(8,128)(2,1)S(1)} %constant_dynamic-update-slice_fusion), channel_id=1, source_target_pairs={{0,1},{1,2},{2,3},{3,0},{4,5},{5,6},{6,7},{7,4},{8,9},{9,10},{10,1... | collective-permute-start | bytes 1228808 | tf_op jit(solution)/shard_map/ppermute | solution.py:25
  82.5 0.0 collective-permute-done.3
  82.5 0.0 collective-permute-done.4
  82.5 0.1 pad_maximum_fusion.1
  82.6 4.3 %collective-permute-start.5 = (bf16[4,456,128]{2,1,0:T(8,128)(2,1)S(1)}, bf16[4,456,128]{2,1,0:T(8,128)(2,1)S(1)}, u32[]{:S(2)}, u32[]{:S(2)}) collective-permute-start(bf16[4,456,128]{2,1,0:T(8,128)(2,1)S(1)} %pad_maximum_fusion.1), channel_id=1, source_target_pairs={{0,3},{1,0},{2,1},{3,2},{4,7},{5,4},{6,5},{7,6},{8,11},{9,8},{10,9... | collective-permute-start | bytes 1400840 | tf_op jit(solution)/shard_map/ppermute | solution.py:25
  86.8 1.9 %collective-permute-start.6 = (bf16[4,456,128]{2,1,0:T(8,128)(2,1)S(1)}, bf16[4,456,128]{2,1,0:T(8,128)(2,1)S(1)}, u32[]{:S(2)}, u32[]{:S(2)}) collective-permute-start(bf16[4,456,128]{2,1,0:T(8,128)(2,1)S(1)} %pad_maximum_fusion.1), channel_id=1, source_target_pairs={{0,2},{1,3},{2,0},{3,1},{4,6},{5,7},{6,4},{7,5},{8,10},{9,11},{10,... | collective-permute-start | bytes 1400840 | tf_op jit(solution)/shard_map/ppermute | solution.py:25
  88.8 0.0 collective-permute-done.11
  88.8 2.5 %collective-permute-start.7 = (bf16[4,456,128]{2,1,0:T(8,128)(2,1)S(1)}, bf16[4,456,128]{2,1,0:T(8,128)(2,1)S(1)}, u32[]{:S(2)}, u32[]{:S(2)}) collective-permute-start(bf16[4,456,128]{2,1,0:T(8,128)(2,1)S(1)} %pad_maximum_fusion.1), channel_id=1, source_target_pairs={{0,1},{1,2},{2,3},{3,0},{4,5},{5,6},{6,7},{7,4},{8,9},{9,10},{10,1... | collective-permute-start | bytes 1400840 | tf_op jit(solution)/shard_map/ppermute | solution.py:25
  91.3 0.0 collective-permute-done.12
  91.3 9.7 %collective-permute-done.13 = bf16[1600,128]{1,0:T(8,128)(2,1)S(1)} collective-permute-done((bf16[1600,128]{1,0:T(8,128)(2,1)S(1)}, bf16[1600,128]{1,0:T(8,128)(2,1)S(1)}, u32[]{:S(2)}, u32[]{:S(2)}) %collective-permute-start.13) | collective-permute-done | bytes 409632 | tf_op jit(solution)/shard_map/ppermute | solution.py:25
  100.9 8.6 %rotate_edges.1 = (bf16[1152,2176]{1,0:T(8,128)(2,1)S(1)}, bf16[9,7,96,256]{3,2,1,0:T(8,128)(2,1)S(1)}) custom-call(s32[256]{0:T(256)S(1)} %fusion.4.slot_ref, s32[1152]{0:T(1024)S(1)} %reduce.1.neighbour_ref, bf16[8,25,8,128]{3,2,1,0:T(8,128)(2,1)S(1)} %bitcast.49, bf16[8,25,8,128]{3,2,1,0:T(8,128)(2,1)S(1)} %bitcast.53, ...), custom_call_target="tpu_custom_call" | custom-call | tf_op jit(solution)/shard_map/rotate_edges/pallas_call | solution.py:199
  109.5 0.1 pad_maximum_fusion.refs_1_
  109.6 0.0 collective-permute-done.5
  109.6 0.0 collective-permute-done.6
  109.6 9.5 %collective-permute-done.7 = bf16[4,456,128]{2,1,0:T(8,128)(2,1)S(1)} collective-permute-done((bf16[4,456,128]{2,1,0:T(8,128)(2,1)S(1)}, bf16[4,456,128]{2,1,0:T(8,128)(2,1)S(1)}, u32[]{:S(2)}, u32[]{:S(2)}) %collective-permute-start.7) | collective-permute-done | bytes 466976 | tf_op jit(solution)/shard_map/ppermute | solution.py:25
  119.1 5.8 %convolve_edges.1 = bf16[25,16,128]{2,1,0:T(8,128)(2,1)} custom-call(s32[2]{0:T(128)S(1)} %pad_add_fusion.refs_0_, bf16[4,57,8,128]{3,2,1,0:T(8,128)(2,1)S(1)} %pad_maximum_fusion.refs_1_, bf16[4,57,8,128]{3,2,1,0:T(8,128)(2,1)S(1)} %bitcast.50, bf16[4,57,8,128]{3,2,1,0:T(8,128)(2,1)S(1)} %bitcast.51, bf16[4,57,8,128]{3,2,1,0:T(8,128)(2,1)S(1)} %bitcast.52, ...), custom_call_target="tpu_custom_call" | custom-call | tf_op jit(solution)/shard_map/convolve_edges/pallas_call | solution.py:296
  (13 shorter events, 0.3 us)
Async XLA Ops:
  0.0 13.1 %copy-start.2 = (f32[32,32]{1,0:T(8,128)S(1)}, f32[32,32]{1,0:T(8,128)}, u32[]{:S(2)}) copy-start(f32[32,32]{1,0:T(8,128)} %param.15) | copy-start | bytes 12292
  0.0 13.5 %copy-start = (bf16[1,13,25,1152]{3,1,2,0:T(8,128)(2,1)S(1)}, bf16[1,13,25,1152]{3,1,2,0:T(8,128)(2,1)}, u32[]{:S(2)}) copy-start(bf16[1,13,25,1152]{3,1,2,0:T(8,128)(2,1)} %param.14) | copy-start | bytes 2246404
  2.2 11.4 %copy-start.4 = (f32[1,1152]{1,0:T(1,128)S(1)}, f32[1,1152]{1,0:T(1,128)}, u32[]{:S(2)}) copy-start(f32[1,1152]{1,0:T(1,128)} %param.13) | copy-start | bytes 13828
  2.2 11.4 %copy-start.5 = (s32[1,1152]{1,0:T(1,128)S(1)}, s32[1,1152]{1,0:T(1,128)}, u32[]{:S(2)}) copy-start(s32[1,1152]{1,0:T(1,128)} %param.12) | copy-start | bytes 13828
  2.2 37.6 %all-to-all-start = ((bf16[8,456,128]{2,1,0:T(8,128)(2,1)}), bf16[8,456,128]{2,1,0:T(8,128)(2,1)S(1)}, u32[]{:S(2)}, u32[]{:S(2)}) async-start(bf16[8,456,128]{2,1,0:T(8,128)(2,1)} %bitcast.59), calls=%async_computation | async-start | bytes 1867776 | tf_op jit(solution)/shard_map/all_to_all | solution.py:339
  13.9 0.7 copy-start.3
  13.9 0.8 copy-start.6
  14.0 29.4 %copy-start.1 = (bf16[1,16,25,128]{3,1,2,0:T(8,128)(2,1)S(1)}, bf16[1,16,25,128]{3,1,2,0:T(8,128)(2,1)}, u32[]{:S(2)}) copy-start(bf16[1,16,25,128]{3,1,2,0:T(8,128)(2,1)} %param.9) | copy-start | bytes 307204
  41.0 12.1 %collective-permute-start = (bf16[2,456,128]{2,1,0:T(8,128)(2,1)S(1)}, bf16[2,456,128]{2,1,0:T(8,128)(2,1)S(1)}, u32[]{:S(2)}, u32[]{:S(2)}) collective-permute-start(bf16[2,456,128]{2,1,0:T(8,128)(2,1)S(1)} %bitcast.57), channel_id=1, source_target_pairs={{0,16},{16,0},{1,17},{17,1},{2,18},{18,2},{3,19},{19,3},{4,20},{20... | collective-permute-start | bytes 700424 | tf_op jit(solution)/shard_map/ppermute | solution.py:25
  43.5 9.5 %collective-permute-start.8 = (bf16[400,128]{1,0:T(8,128)(2,1)S(1)}, bf16[400,128]{1,0:T(8,128)(2,1)S(1)}, u32[]{:S(2)}, u32[]{:S(2)}) collective-permute-start(bf16[400,128]{1,0:T(8,128)(2,1)S(1)} %reshape_squeeze.3), channel_id=1, source_target_pairs={{0,12},{4,0},{8,4},{12,8},{1,13},{5,1},{9,5},{13,9},{2,14},{6,2},{... | collective-permute-start | bytes 307208 | tf_op jit(solution)/shard_map/ppermute | solution.py:25
  48.7 10.1 %collective-permute-start.9 = (bf16[400,128]{1,0:T(8,128)(2,1)S(1)}, bf16[400,128]{1,0:T(8,128)(2,1)S(1)}, u32[]{:S(2)}, u32[]{:S(2)}) collective-permute-start(bf16[400,128]{1,0:T(8,128)(2,1)S(1)} %reshape_squeeze.3), channel_id=1, source_target_pairs={{0,8},{4,12},{8,0},{12,4},{1,9},{5,13},{9,1},{13,5},{2,10},{6,14},... | collective-permute-start | bytes 307208 | tf_op jit(solution)/shard_map/ppermute | solution.py:25
  50.7 8.2 %collective-permute-start.10 = (bf16[400,128]{1,0:T(8,128)(2,1)S(1)}, bf16[400,128]{1,0:T(8,128)(2,1)S(1)}, u32[]{:S(2)}, u32[]{:S(2)}) collective-permute-start(bf16[400,128]{1,0:T(8,128)(2,1)S(1)} %reshape_squeeze.3), channel_id=1, source_target_pairs={{0,4},{4,8},{8,12},{12,0},{1,5},{5,9},{9,13},{13,1},{2,6},{6,10},{... | collective-permute-start | bytes 307208 | tf_op jit(solution)/shard_map/ppermute | solution.py:25
  53.1 10.1 %collective-permute-start.1 = (bf16[456,128]{1,0:T(8,128)(2,1)S(1)}, bf16[456,128]{1,0:T(8,128)(2,1)S(1)}, u32[]{:S(2)}, u32[]{:S(2)}) collective-permute-start(bf16[456,128]{1,0:T(8,128)(2,1)S(1)} %fusion), channel_id=1, source_target_pairs={{0,256},{256,0},{1,257},{257,1},{2,258},{258,2},{3,259},{259,3},{4... | collective-permute-start | bytes 350216 | tf_op jit(solution)/shard_map/ppermute | solution.py:25
  58.8 29.9 %collective-permute-start.11 = (bf16[1600,128]{1,0:T(8,128)(2,1)S(1)}, bf16[1600,128]{1,0:T(8,128)(2,1)S(1)}, u32[]{:S(2)}, u32[]{:S(2)}) collective-permute-start(bf16[1600,128]{1,0:T(8,128)(2,1)S(1)} %constant_dynamic-update-slice_fusion), channel_id=1, source_target_pairs={{0,3},{1,0},{2,1},{3,2},{4,7},{5,4},{6,5},{7,6},{8,11},{9,8},{10,9... | collective-permute-start | bytes 1228808 | tf_op jit(solution)/shard_map/ppermute | solution.py:25
  63.3 16.9 %collective-permute-start.2 = (bf16[456,128]{1,0:T(8,128)(2,1)S(1)}, bf16[456,128]{1,0:T(8,128)(2,1)S(1)}, u32[]{:S(2)}, u32[]{:S(2)}) collective-permute-start(bf16[456,128]{1,0:T(8,128)(2,1)S(1)} %add_convert_fusion), channel_id=1, source_target_pairs={{0,12},{4,0},{8,4},{12,8},{1,13},{5,1},{9,5},{13,9},{2,14},{6,2},{... | collective-permute-start | bytes 350216 | tf_op jit(solution)/shard_map/ppermute | solution.py:25
  68.1 14.4 %collective-permute-start.3 = (bf16[456,128]{1,0:T(8,128)(2,1)S(1)}, bf16[456,128]{1,0:T(8,128)(2,1)S(1)}, u32[]{:S(2)}, u32[]{:S(2)}) collective-permute-start(bf16[456,128]{1,0:T(8,128)(2,1)S(1)} %add_convert_fusion), channel_id=1, source_target_pairs={{0,8},{4,12},{8,0},{12,4},{1,9},{5,13},{9,1},{13,5},{2,10},{6,14},... | collective-permute-start | bytes 350216 | tf_op jit(solution)/shard_map/ppermute | solution.py:25
  72.7 9.8 %collective-permute-start.4 = (bf16[456,128]{1,0:T(8,128)(2,1)S(1)}, bf16[456,128]{1,0:T(8,128)(2,1)S(1)}, u32[]{:S(2)}, u32[]{:S(2)}) collective-permute-start(bf16[456,128]{1,0:T(8,128)(2,1)S(1)} %add_convert_fusion), channel_id=1, source_target_pairs={{0,4},{4,8},{8,12},{12,0},{1,5},{5,9},{9,13},{13,1},{2,6},{6,10},{... | collective-permute-start | bytes 350216 | tf_op jit(solution)/shard_map/ppermute | solution.py:25
  75.6 15.7 %collective-permute-start.12 = (bf16[1600,128]{1,0:T(8,128)(2,1)S(1)}, bf16[1600,128]{1,0:T(8,128)(2,1)S(1)}, u32[]{:S(2)}, u32[]{:S(2)}) collective-permute-start(bf16[1600,128]{1,0:T(8,128)(2,1)S(1)} %constant_dynamic-update-slice_fusion), channel_id=1, source_target_pairs={{0,2},{1,3},{2,0},{3,1},{4,6},{5,7},{6,4},{7,5},{8,10},{9,11},{10,... | collective-permute-start | bytes 1228808 | tf_op jit(solution)/shard_map/ppermute | solution.py:25
  80.2 20.7 %collective-permute-start.13 = (bf16[1600,128]{1,0:T(8,128)(2,1)S(1)}, bf16[1600,128]{1,0:T(8,128)(2,1)S(1)}, u32[]{:S(2)}, u32[]{:S(2)}) collective-permute-start(bf16[1600,128]{1,0:T(8,128)(2,1)S(1)} %constant_dynamic-update-slice_fusion), channel_id=1, source_target_pairs={{0,1},{1,2},{2,3},{3,0},{4,5},{5,6},{6,7},{7,4},{8,9},{9,10},{10,1... | collective-permute-start | bytes 1228808 | tf_op jit(solution)/shard_map/ppermute | solution.py:25
  82.6 27.0 %collective-permute-start.5 = (bf16[4,456,128]{2,1,0:T(8,128)(2,1)S(1)}, bf16[4,456,128]{2,1,0:T(8,128)(2,1)S(1)}, u32[]{:S(2)}, u32[]{:S(2)}) collective-permute-start(bf16[4,456,128]{2,1,0:T(8,128)(2,1)S(1)} %pad_maximum_fusion.1), channel_id=1, source_target_pairs={{0,3},{1,0},{2,1},{3,2},{4,7},{5,4},{6,5},{7,6},{8,11},{9,8},{10,9... | collective-permute-start | bytes 1400840 | tf_op jit(solution)/shard_map/ppermute | solution.py:25
  86.8 22.8 %collective-permute-start.6 = (bf16[4,456,128]{2,1,0:T(8,128)(2,1)S(1)}, bf16[4,456,128]{2,1,0:T(8,128)(2,1)S(1)}, u32[]{:S(2)}, u32[]{:S(2)}) collective-permute-start(bf16[4,456,128]{2,1,0:T(8,128)(2,1)S(1)} %pad_maximum_fusion.1), channel_id=1, source_target_pairs={{0,2},{1,3},{2,0},{3,1},{4,6},{5,7},{6,4},{7,5},{8,10},{9,11},{10,... | collective-permute-start | bytes 1400840 | tf_op jit(solution)/shard_map/ppermute | solution.py:25
  88.8 30.4 %collective-permute-start.7 = (bf16[4,456,128]{2,1,0:T(8,128)(2,1)S(1)}, bf16[4,456,128]{2,1,0:T(8,128)(2,1)S(1)}, u32[]{:S(2)}, u32[]{:S(2)}) collective-permute-start(bf16[4,456,128]{2,1,0:T(8,128)(2,1)S(1)} %pad_maximum_fusion.1), channel_id=1, source_target_pairs={{0,1},{1,2},{2,3},{3,0},{4,5},{5,6},{6,7},{7,4},{8,9},{9,10},{10,1... | collective-permute-start | bytes 1400840 | tf_op jit(solution)/shard_map/ppermute | solution.py:25

commit v4 on v3

--- a/solution.py
+++ b/solution.py
@@ -124,13 +124,51 @@
                 ] = jnp.where(inside, w, jnp.zeros_like(w))
 
 
+def frames_kernel(wigner_ref, rows_ref):
+    frame = wigner_ref.shape[0]
+    width = GROUP * PAD
+    block = wigner_ref.shape[2]
+    column = lax.broadcasted_iota(jnp.int32, (PAD, width), 1)
+    row = lax.broadcasted_iota(jnp.int32, (PAD, width), 0)
+    repeat = (column % PAD == row).astype(jnp.bfloat16)
+    edge = lax.broadcasted_iota(jnp.int32, (block, width), 0)
+    lane = lax.broadcasted_iota(jnp.int32, (block, width), 1)
+    own = edge % GROUP == lane // PAD
+    for r0 in range(0, frame, 2):
+        parts = []
+        for r in range(r0, min(r0 + 2, frame)):
+            part = lax.dot_general(
+                wigner_ref[r],
+                repeat,
+                (((0,), (0,)), ((), ())),
+                preferred_element_type=jnp.float32,
+            )
+            parts.append(jnp.where(own, part, 0.0))
+        for g in range(block // GROUP):
+            low = g * GROUP
+            tiles = [p[low : low + GROUP] for p in parts]
+            tile = tiles[0] if len(tiles) == 1 else jnp.concatenate(tiles, axis=0)
+            rows_ref[g, r0 * GROUP : r0 * GROUP + tile.shape[0]] = tile.astype(jnp.bfloat16)
+
+
+def frames(wigner):
+    frame, pad, edges = wigner.shape
+    return pl.pallas_call(
+        frames_kernel,
+        grid=(edges // LANES,),
+        out_shape=jax.ShapeDtypeStruct((edges // GROUP, frame * GROUP, GROUP * PAD), jnp.bfloat16),
+        in_specs=[pl.BlockSpec((frame, pad, LANES), lambda b: (0, 0, b))],
+        out_specs=pl.BlockSpec((LANES // GROUP, frame * GROUP, GROUP * PAD), lambda b: (b, 0, 0)),
+        name="spread_frames",
+    )(wigner)
+
+
 def rotate_kernel(slot_ref, neighbour_ref, *refs):
     piece_refs = refs[:4]
-    wigner_ref, gated_ref, out_ref, picked_ref, feature_ref, row_ref, spread_ref = refs[4:]
-    frame = wigner_ref.shape[0]
-    pick_atoms(gated_ref, picked_ref)
+    gated_ref, rows_ref, out_ref, picked_ref, feature_ref, row_ref = refs[4:]
+    step = pl.program_id(0)
+    frame = rows_ref.shape[1] // GROUP
     runs, harmonics = piece_refs[0].shape[:2]
-    row_ref[:, 8 * harmonics :] = jnp.zeros_like(row_ref[:, 8 * harmonics :])
 
     def eight_atoms(run, carry):
         for k, ref in enumerate(piece_refs):
@@ -140,64 +178,49 @@
                 feature_ref[(k * runs + run) * 8 + a] = rows.astype(jnp.bfloat16)
         return carry
 
-    lax.fori_loop(0, runs, eight_atoms, 0)
-    width = GROUP * PAD
-    block = LANES
-    column = lax.broadcasted_iota(jnp.int32, (PAD, width), 1)
-    row = lax.broadcasted_iota(jnp.int32, (PAD, width), 0)
-    repeat = (column % PAD == row).astype(jnp.bfloat16)
-    edge = lax.broadcasted_iota(jnp.int32, (block, width), 0)
-    lane = lax.broadcasted_iota(jnp.int32, (block, width), 1)
-    own = edge % GROUP == lane // PAD
-
-    def one_block(b, carry):
-        start = pl.multiple_of(b * block, block)
+    @pl.when(step == 0)
+    def _():
+        pick_atoms(gated_ref, picked_ref)
+        row_ref[:, 8 * harmonics :] = jnp.zeros_like(row_ref[:, 8 * harmonics :])
+        lax.fori_loop(0, runs, eight_atoms, 0)
+
+    for pair in range(rows_ref.shape[0] // 2):
+        low = pair * 2 * GROUP
+        start = step * LANES + low
+        halves = []
+        for half in range(2):
+            tiles = []
+            for e in range(GROUP):
+                source = slot_ref[neighbour_ref[start + half * GROUP + e]]
+                tiles.append(feature_ref[source])
+            halves.append(
+                lax.dot_general(
+                    rows_ref[2 * pair + half],
+                    jnp.concatenate(tiles, axis=0),
+                    (((1,), (0,)), ((), ())),
+                    preferred_element_type=jnp.float32,
+                )
+            )
+        rows = slice(low, low + 2 * GROUP)
+        both = []
         for r in range(frame):
-            part = lax.dot_general(
-                wigner_ref[r, :, pl.ds(start, block)],
-                repeat,
-                (((0,), (0,)), ((), ())),
-                preferred_element_type=jnp.float32,
-            )
-            spread_ref[r] = jnp.where(own, part, 0.0)
-        for pair in range(block // (2 * GROUP)):
-            halves = []
-            for half in range(2):
-                low = (2 * pair + half) * GROUP
-                tiles = []
-                for e in range(GROUP):
-                    source = slot_ref[neighbour_ref[start + low + e]]
-                    tiles.append(feature_ref[source])
-                stacked = jnp.concatenate(tiles, axis=0)
-                rows = jnp.concatenate(
-                    [spread_ref[r, low : low + GROUP, :] for r in range(frame)], axis=0
-                ).astype(jnp.bfloat16)
-                halves.append(
-                    lax.dot_general(
-                        rows, stacked, (((1,), (0,)), ((), ())), preferred_element_type=jnp.float32
-                    )
-                )
-            rows = pl.ds(pl.multiple_of(start + 2 * GROUP * pair, 2 * GROUP), 2 * GROUP)
-            both = []
-            for r in range(frame):
-                tile = jnp.concatenate([h[GROUP * r : GROUP * (r + 1)] for h in halves], axis=0)
-                tile = tile.astype(out_ref.dtype)
-                out_ref[rows, r * LANES : (r + 1) * LANES] = tile
-                both.append(tile.astype(jnp.float32))
-            for m in range(LMAX):
-                tile = both[LMAX + 1 + m] + both[2 * LMAX + 1 + m]
-                out_ref[rows, (frame + m) * LANES : (frame + m + 1) * LANES] = tile.astype(out_ref.dtype)
-        return carry
-
-    lax.fori_loop(0, neighbour_ref.shape[0] // block, one_block, 0)
-
-
-def rotate(slots, neighbour, pieces, wigner, gated):
-    frame, _, edges = wigner.shape
+            tile = jnp.concatenate([h[GROUP * r : GROUP * (r + 1)] for h in halves], axis=0)
+            tile = tile.astype(out_ref.dtype)
+            out_ref[rows, r * LANES : (r + 1) * LANES] = tile
+            both.append(tile.astype(jnp.float32))
+        for m in range(LMAX):
+            tile = both[LMAX + 1 + m] + both[2 * LMAX + 1 + m]
+            out_ref[rows, (frame + m) * LANES : (frame + m + 1) * LANES] = tile.astype(out_ref.dtype)
+
+
+def rotate(slots, neighbour, pieces, gated, rows):
+    frame = rows.shape[1] // GROUP
+    edges = neighbour.shape[0]
     runs, harmonics = pieces[0].shape[:2]
     atoms = len(pieces) * runs * 8
     return pl.pallas_call(
         rotate_kernel,
+        grid=(edges // LANES,),
         out_shape=(
             jax.ShapeDtypeStruct((edges, (frame + LMAX) * LANES), jnp.bfloat16),
             jax.ShapeDtypeStruct((edges // LANES, (frame + 1) // 2, 3 * PAD, 2 * LANES), jnp.bfloat16),
@@ -206,43 +229,48 @@
             pl.BlockSpec(memory_space=pltpu.SMEM),
             pl.BlockSpec(memory_space=pltpu.SMEM),
         ]
-        + [pl.BlockSpec(memory_space=pltpu.VMEM)] * (len(pieces) + 2),
-        out_specs=(pl.BlockSpec(memory_space=pltpu.VMEM), pl.BlockSpec(memory_space=pltpu.VMEM)),
+        + [pl.BlockSpec(memory_space=pltpu.VMEM)] * (len(pieces) + 1)
+        + [pl.BlockSpec((LANES // GROUP, *rows.shape[1:]), lambda b: (b, 0, 0))],
+        out_specs=(
+            pl.BlockSpec((LANES, (frame + LMAX) * LANES), lambda b: (b, 0)),
+            pl.BlockSpec(memory_space=pltpu.VMEM),
+        ),
         scratch_shapes=[
             pltpu.VMEM((atoms, PAD, LANES), jnp.bfloat16),
             pltpu.VMEM((len(pieces), 8 * harmonics + 8, LANES), jnp.float32),
-            pltpu.VMEM((frame, LANES, GROUP * PAD), jnp.float32),
         ],
-        compiler_params=pltpu.CompilerParams(vmem_limit_bytes=26 * MIB),
+        compiler_params=pltpu.CompilerParams(vmem_limit_bytes=40 * MIB),
         name="rotate_edges",
-    )(slots, neighbour, *pieces, wigner, gated)
+    )(slots, neighbour, *pieces, gated, rows)
 
 
 def convolve_kernel(zero_shape, one_shape, x_ref, *refs):
     xs = 4
-    column_refs = refs[:xs]
-    rotated_ref, picked_ref, out_ref, zero32, one32, zero16, real16, sum16, diff16, message, total = refs[xs:]
+    column_refs = refs[: 2 * xs]
+    rotated_ref, picked_ref, out_ref, zero32, one32, zero16, real16, sum16, diff16, message, total = refs[2 * xs :]
     zero_rows, zero_width = zero_shape
     parts, one_rows, one_width = one_shape
-    ys = column_refs[0].shape[0]
+    half = column_refs[0].shape[0]
+    ys = 2 * half
     zero_tiles, one_tiles = zero_width // LANES, one_width // LANES
     for k in range(xs):
         place = (x_ref[1] + k) % xs
         for y in range(ys):
             g = (x_ref[0] + y) % ys * xs + place
+            piece_ref = column_refs[2 * k + y // half].at[y % half]
             for i in range(zero_rows // 8):
                 at = pl.multiple_of(g * zero_rows + 8 * i, 8)
                 for t in range(zero_tiles):
-                    zero32[pl.ds(at, 8), t * LANES : (t + 1) * LANES] = column_refs[k][
-                        y, i * zero_tiles + t
+                    zero32[pl.ds(at, 8), t * LANES : (t + 1) * LANES] = piece_ref[
+                        i * zero_tiles + t
                     ].astype(jnp.float32)
             first = zero_rows // 8 * zero_tiles
             for p in range(parts):
                 for i in range(one_rows // 8):
                     at = pl.multiple_of(g * one_rows + 8 * i, 8)
                     for t in range(one_tiles):
-                        one32[p, pl.ds(at, 8), t * LANES : (t + 1) * LANES] = column_refs[k][
-                            y, first + (p * (one_rows // 8) + i) * one_tiles + t
+                        one32[p, pl.ds(at, 8), t * LANES : (t + 1) * LANES] = piece_ref[
+                            first + (p * (one_rows // 8) + i) * one_tiles + t
                         ].astype(jnp.float32)
     zero16[...] = zero32[...].astype(jnp.bfloat16)
     real16[...] = one32[0].astype(jnp.bfloat16)
@@ -362,8 +390,9 @@
     table = jnp.where(yh == 0, table, table[::-1])
     factors = jnp.where(c == 0, table, table[:, ::-1]).reshape(4, zs)
     there = jnp.stack([y, x])
-    wigner, gated, slots, edges_from, chunks, factors, there = lax.optimization_barrier(
-        (wigner, gated, slots, edges_from, chunks, factors, there)
+    rows = frames(wigner)
+    rows, gated, slots, edges_from, chunks, factors, there = lax.optimization_barrier(
+        (rows, gated, slots, edges_from, chunks, factors, there)
     )
     send, other, own = partial_sums(factors, chunks)
     swapped = turned(send, "c", 1)
@@ -374,14 +403,17 @@
     column = [merged]
     for k in range(1, ys):
         column.append(turned(merged, "yl", -k))
-    column = jnp.stack(column)
-    columns = [column] * xs
-    for k in FAR_FIRST:
-        columns[k] = turned(column, "x", -k)
-    rotated, gathered = rotate(slots, edges_from, pieces, wigner, gated)
+    halves = [jnp.stack(column[: ys // 2]), jnp.stack(column[ys // 2 :])]
+    columns = {(0, half): rows for half, rows in enumerate(halves)}
+    for half, by in ((0, 1), (0, 3), (1, 3), (1, 1)):
+        columns[by, half] = turned(halves[half], "x", -by)
+    for half, by in ((0, 1), (1, 3)):
+        columns[2, half] = turned(columns[by, half], "x", -by)
+    columns = [columns[k, half] for k in range(xs) for half in range(2)]
+    rotated, gathered = rotate(slots, edges_from, pieces, gated, rows)
     update = convolve(
         there,
-        [m.reshape(ys, -1, 8, LANES) for m in columns],
+        [m.reshape(ys // 2, -1, 8, LANES) for m in columns],
         rotated,
         gathered,
         (zero_rows, zero_width),

time: 126 us -> 134 us (1.063)
  the two profiles are of different devices: /device:TPU:1 before, /device:TPU:6 now
where the time goes in v4:
time: 134 us; the launch traced here: 132 us
  starting transfers between devices  71.2 us (53%)
  waiting for transfers between devices  30.7 us (23%)
  Pallas kernels  26.5 us (20%)
  local copies, waits for them, and re-layouts  2.92 us (2%)
    ppermute x17, starting transfers between devices, turned(): lax.ppermute(value, axis, [(i, (i + by) % size) for i in range(size)])  60.9 us
    ppermute x17, waiting for transfers between devices, turned(): lax.ppermute(value, axis, [(i, (i + by) % size) for i in range(size)])  16.1 us
    all_to_all x1, waiting for transfers between devices, shards(): chunks = lax.all_to_all(copies, 'z', 0, 0, tiled=True)  14.6 us
    all_to_all x1, starting transfers between devices, shards(): chunks = lax.all_to_all(copies, 'z', 0, 0, tiled=True)  10.3 us
    pallas_call x1, Pallas kernels, rotate(): pl.pallas_call(rotate_kernel, grid=(edges // LANES,), out_shape=(jax.Shap...  8.85 us
    pallas_call x1, Pallas kernels, frames(): pl.pallas_call(frames_kernel, grid=(edges // LANES,), out_shape=jax.Shape...  8.44 us
    pallas_call x1, Pallas kernels, convolve(): pl.pallas_call(lambda *refs: convolve_kernel(zero_shape, one_shape, *refs...  5.8 us
  transfers between devices with their start and end apart: 18, of which 6 were waited for; matrix products, arithmetic and copies ran while one was open for 2% of the time, Pallas kernels for 13%

profile of v4, /device:TPU:6, one launch (start us, length us, event | category | flops | bytes accessed | tf_op | source)
XLA Modules:
  0.0 132.3 jit_solution(12333264300029751787)
XLA Ops:
  0.0 0.0 copy-start
  0.0 2.3 %spread_weights.1 = bf16[8,57,8,128]{3,2,1,0:T(8,128)(2,1)} custom-call(bf16[40,640]{1,0:T(8,128)(2,1)} %bitcast.75, bf16[32,2,512]{2,1,0:T(2,128)(2,1)} %bitcast.74), custom_call_target="tpu_custom_call" | custom-call | tf_op jit(solution)/shard_map/spread_weights/pallas_call | solution.py:57
  2.3 10.3 %all-to-all-start = ((bf16[8,456,128]{2,1,0:T(8,128)(2,1)}), bf16[8,456,128]{2,1,0:T(8,128)(2,1)S(1)}, u32[]{:S(2)}, u32[]{:S(2)}) async-start(bf16[8,456,128]{2,1,0:T(8,128)(2,1)} %bitcast.65), calls=%async_computation | async-start | bytes 1867776 | tf_op jit(solution)/shard_map/all_to_all | solution.py:367
  12.6 0.9 reshape.81
  13.5 0.2 dynamic-slice_reduce_fusion
  13.7 0.0 copy-done
  13.7 0.2 copy.19
  13.9 1.1 pad.7.wigner_ref
  15.0 0.0 copy-start.3
  15.0 0.0 copy-start.4
  15.0 8.4 %spread_frames.1.refs_5_ = bf16[144,104,256]{2,1,0:T(8,128)(2,1)} custom-call(bf16[13,32,1152]{2,1,0:T(8,128)(2,1)} %pad.7.wigner_ref), custom_call_target="tpu_custom_call" | custom-call | tf_op jit(solution)/shard_map/spread_frames/pallas_call | solution.py:156
  23.4 0.0 copy-done.3
  23.4 0.0 copy-done.4
  23.4 0.0 copy-start.2
  23.5 0.0 copy-start.5
  23.5 0.0 copy-start.1
  23.5 0.2 multiply_convert_fusion
  23.7 0.1 pad.8.refs_4_
  23.8 0.3 copy-done.2
  24.2 0.1 pad_add_fusion.refs_0_
  24.2 0.0 copy-done.5
  24.3 14.6 %all-to-all-done = bf16[8,456,128]{2,1,0:T(8,128)(2,1)S(1)} async-done(((bf16[8,456,128]{2,1,0:T(8,128)(2,1)}), bf16[8,456,128]{2,1,0:T(8,128)(2,1)S(1)}, u32[]{:S(2)}, u32[]{:S(2)}) %all-to-all-start) | async-done | bytes 933920 | tf_op jit(solution)/shard_map/all_to_all | solution.py:367
  38.9 1.1 merge_experts.1
  40.0 1.9 %collective-permute-start = (bf16[2,456,128]{2,1,0:T(8,128)(2,1)S(1)}, bf16[2,456,128]{2,1,0:T(8,128)(2,1)S(1)}, u32[]{:S(2)}, u32[]{:S(2)}) collective-permute-start(bf16[2,456,128]{2,1,0:T(8,128)(2,1)S(1)} %bitcast.63), channel_id=1, source_target_pairs={{0,16},{16,0},{1,17},{17,1},{2,18},{18,2},{3,19},{19,3},{4,20},{20... | collective-permute-start | bytes 700424 | tf_op jit(solution)/shard_map/ppermute | solution.py:25
  42.0 0.0 copy-done.1
  42.1 5.5 %collective-permute-start.11 = (bf16[400,128]{1,0:T(8,128)(2,1)S(1)}, bf16[400,128]{1,0:T(8,128)(2,1)S(1)}, u32[]{:S(2)}, u32[]{:S(2)}) collective-permute-start(bf16[400,128]{1,0:T(8,128)(2,1)S(1)} %reshape_squeeze.3), channel_id=1, source_target_pairs={{0,12},{4,0},{8,4},{12,8},{1,13},{5,1},{9,5},{13,9},{2,14},{6,2},{... | collective-permute-start | bytes 307208 | tf_op jit(solution)/shard_map/ppermute | solution.py:25
  47.6 1.9 %collective-permute-start.12 = (bf16[400,128]{1,0:T(8,128)(2,1)S(1)}, bf16[400,128]{1,0:T(8,128)(2,1)S(1)}, u32[]{:S(2)}, u32[]{:S(2)}) collective-permute-start(bf16[400,128]{1,0:T(8,128)(2,1)S(1)} %reshape_squeeze.3), channel_id=1, source_target_pairs={{0,8},{4,12},{8,0},{12,4},{1,9},{5,13},{9,1},{13,5},{2,10},{6,14},... | collective-permute-start | bytes 307208 | tf_op jit(solution)/shard_map/ppermute | solution.py:25
  49.5 2.9 %collective-permute-start.13 = (bf16[400,128]{1,0:T(8,128)(2,1)S(1)}, bf16[400,128]{1,0:T(8,128)(2,1)S(1)}, u32[]{:S(2)}, u32[]{:S(2)}) collective-permute-start(bf16[400,128]{1,0:T(8,128)(2,1)S(1)} %reshape_squeeze.3), channel_id=1, source_target_pairs={{0,4},{4,8},{8,12},{12,0},{1,5},{5,9},{9,13},{13,1},{2,6},{6,10},{... | collective-permute-start | bytes 307208 | tf_op jit(solution)/shard_map/ppermute | solution.py:25
  52.4 0.0 collective-permute-done
  52.5 5.9 %collective-permute-start.1 = (bf16[456,128]{1,0:T(8,128)(2,1)S(1)}, bf16[456,128]{1,0:T(8,128)(2,1)S(1)}, u32[]{:S(2)}, u32[]{:S(2)}) collective-permute-start(bf16[456,128]{1,0:T(8,128)(2,1)S(1)} %fusion), channel_id=1, source_target_pairs={{0,256},{256,0},{1,257},{257,1},{2,258},{258,2},{3,259},{259,3},{4... | collective-permute-start | bytes 350216 | tf_op jit(solution)/shard_map/ppermute | solution.py:25
  58.4 0.0 collective-permute-done.11
  58.5 4.7 %collective-permute-done.1 = bf16[456,128]{1,0:T(8,128)(2,1)S(1)} collective-permute-done((bf16[456,128]{1,0:T(8,128)(2,1)S(1)}, bf16[456,128]{1,0:T(8,128)(2,1)S(1)}, u32[]{:S(2)}, u32[]{:S(2)}) %collective-permute-start.1) | collective-permute-done | bytes 116768 | tf_op jit(solution)/shard_map/ppermute | solution.py:25
  63.1 0.1 add_convert_fusion
  63.2 6.5 %collective-permute-start.3 = (bf16[456,128]{1,0:T(8,128)(2,1)S(1)}, bf16[456,128]{1,0:T(8,128)(2,1)S(1)}, u32[]{:S(2)}, u32[]{:S(2)}) collective-permute-start(bf16[456,128]{1,0:T(8,128)(2,1)S(1)} %add_convert_fusion), channel_id=1, source_target_pairs={{0,8},{4,12},{8,0},{12,4},{1,9},{5,13},{9,1},{13,5},{2,10},{6,14},... | collective-permute-start | bytes 350216 | tf_op jit(solution)/shard_map/ppermute | solution.py:25
  69.7 2.6 %collective-permute-start.4 = (bf16[456,128]{1,0:T(8,128)(2,1)S(1)}, bf16[456,128]{1,0:T(8,128)(2,1)S(1)}, u32[]{:S(2)}, u32[]{:S(2)}) collective-permute-start(bf16[456,128]{1,0:T(8,128)(2,1)S(1)} %add_convert_fusion), channel_id=1, source_target_pairs={{0,4},{4,8},{8,12},{12,0},{1,5},{5,9},{9,13},{13,1},{2,6},{6,10},{... | collective-permute-start | bytes 350216 | tf_op jit(solution)/shard_map/ppermute | solution.py:25
  72.3 0.0 collective-permute-done.12
  72.4 0.0 collective-permute-done.13
  72.4 2.7 %collective-permute-start.14 = (bf16[1600,128]{1,0:T(8,128)(2,1)S(1)}, bf16[1600,128]{1,0:T(8,128)(2,1)S(1)}, u32[]{:S(2)}, u32[]{:S(2)}) collective-permute-start(bf16[1600,128]{1,0:T(8,128)(2,1)S(1)} %constant_dynamic-update-slice_fusion), channel_id=1, source_target_pairs={{0,3},{1,0},{2,1},{3,2},{4,7},{5,4},{6,5},{7,6},{8,11},{9,8},{10,9... | collective-permute-start | bytes 1228808 | tf_op jit(solution)/shard_map/ppermute | solution.py:25
  75.2 3.0 %collective-permute-start.15 = (bf16[1600,128]{1,0:T(8,128)(2,1)S(1)}, bf16[1600,128]{1,0:T(8,128)(2,1)S(1)}, u32[]{:S(2)}, u32[]{:S(2)}) collective-permute-start(bf16[1600,128]{1,0:T(8,128)(2,1)S(1)} %constant_dynamic-update-slice_fusion), channel_id=1, source_target_pairs={{0,2},{1,3},{2,0},{3,1},{4,6},{5,7},{6,4},{7,5},{8,10},{9,11},{10,... | collective-permute-start | bytes 1228808 | tf_op jit(solution)/shard_map/ppermute | solution.py:25
  78.2 4.0 %collective-permute-start.16 = (bf16[1600,128]{1,0:T(8,128)(2,1)S(1)}, bf16[1600,128]{1,0:T(8,128)(2,1)S(1)}, u32[]{:S(2)}, u32[]{:S(2)}) collective-permute-start(bf16[1600,128]{1,0:T(8,128)(2,1)S(1)} %constant_dynamic-update-slice_fusion), channel_id=1, source_target_pairs={{0,1},{1,2},{2,3},{3,0},{4,5},{5,6},{6,7},{7,4},{8,9},{9,10},{10,1... | collective-permute-start | bytes 1228808 | tf_op jit(solution)/shard_map/ppermute | solution.py:25
  82.2 0.0 collective-permute-done.3
  82.2 5.0 %collective-permute-start.2 = (bf16[456,128]{1,0:T(8,128)(2,1)S(1)}, bf16[456,128]{1,0:T(8,128)(2,1)S(1)}, u32[]{:S(2)}, u32[]{:S(2)}) collective-permute-start(bf16[456,128]{1,0:T(8,128)(2,1)S(1)} %add_convert_fusion), channel_id=1, source_target_pairs={{0,12},{4,0},{8,4},{12,8},{1,13},{5,1},{9,5},{13,9},{2,14},{6,2},{... | collective-permute-start | bytes 350216 | tf_op jit(solution)/shard_map/ppermute | solution.py:25
  87.2 0.0 collective-permute-done.4
  87.3 2.8 %collective-permute-start.8 = (bf16[2,456,128]{2,1,0:T(8,128)(2,1)S(1)}, bf16[2,456,128]{2,1,0:T(8,128)(2,1)S(1)}, u32[]{:S(2)}, u32[]{:S(2)}) collective-permute-start(bf16[2,456,128]{2,1,0:T(8,128)(2,1)S(1)} %pad_maximum_fusion.3), channel_id=1, source_target_pairs={{0,1},{1,2},{2,3},{3,0},{4,5},{5,6},{6,7},{7,4},{8,9},{9,10},{10,1... | collective-permute-start | bytes 700424 | tf_op jit(solution)/shard_map/ppermute | solution.py:25
  90.1 0.0 collective-permute-done.2
  90.1 3.0 %collective-permute-start.5 = (bf16[2,456,128]{2,1,0:T(8,128)(2,1)S(1)}, bf16[2,456,128]{2,1,0:T(8,128)(2,1)S(1)}, u32[]{:S(2)}, u32[]{:S(2)}) collective-permute-start(bf16[2,456,128]{2,1,0:T(8,128)(2,1)S(1)} %pad_maximum_fusion.2), channel_id=1, source_target_pairs={{0,3},{1,0},{2,1},{3,2},{4,7},{5,4},{6,5},{7,6},{8,11},{9,8},{10,9... | collective-permute-start | bytes 700424 | tf_op jit(solution)/shard_map/ppermute | solution.py:25
  93.2 2.2 %collective-permute-done.14 = bf16[1600,128]{1,0:T(8,128)(2,1)S(1)} collective-permute-done((bf16[1600,128]{1,0:T(8,128)(2,1)S(1)}, bf16[1600,128]{1,0:T(8,128)(2,1)S(1)}, u32[]{:S(2)}, u32[]{:S(2)}) %collective-permute-start.14) | collective-permute-done | bytes 409632 | tf_op jit(solution)/shard_map/ppermute | solution.py:25
  95.4 0.0 collective-permute-done.15
  95.4 4.1 %collective-permute-done.16 = bf16[1600,128]{1,0:T(8,128)(2,1)S(1)} collective-permute-done((bf16[1600,128]{1,0:T(8,128)(2,1)S(1)}, bf16[1600,128]{1,0:T(8,128)(2,1)S(1)}, u32[]{:S(2)}, u32[]{:S(2)}) %collective-permute-start.16) | collective-permute-done | bytes 409632 | tf_op jit(solution)/shard_map/ppermute | solution.py:25
  99.4 8.8 %rotate_edges.1 = (bf16[1152,2176]{1,0:T(8,128)(2,1)S(1)}, bf16[9,7,96,256]{3,2,1,0:T(8,128)(2,1)S(1)}) custom-call(s32[256]{0:T(256)S(1)} %fusion.4.slot_ref, s32[1152]{0:T(1024)S(1)} %reduce.1.neighbour_ref, bf16[8,25,8,128]{3,2,1,0:T(8,128)(2,1)S(1)} %bitcast.52, bf16[8,25,8,128]{3,2,1,0:T(8,128)(2,1)S(1)} %bitcast.53, ...), custom_call_target="tpu_custom_call" | custom-call | tf_op jit(solution)/shard_map/rotate_edges/pallas_call | solution.py:221
  108.3 1.9 %collective-permute-start.6 = (bf16[2,456,128]{2,1,0:T(8,128)(2,1)S(1)}, bf16[2,456,128]{2,1,0:T(8,128)(2,1)S(1)}, u32[]{:S(2)}, u32[]{:S(2)}) collective-permute-start(bf16[2,456,128]{2,1,0:T(8,128)(2,1)S(1)} %pad_maximum_fusion.3), channel_id=1, source_target_pairs={{0,3},{1,0},{2,1},{3,2},{4,7},{5,4},{6,5},{7,6},{8,11},{9,8},{10,9... | collective-permute-start | bytes 700424 | tf_op jit(solution)/shard_map/ppermute | solution.py:25
  110.2 5.1 %collective-permute-start.10 = (bf16[2,456,128]{2,1,0:T(8,128)(2,1)S(1)}, bf16[2,456,128]{2,1,0:T(8,128)(2,1)S(1)}, u32[]{:S(2)}, u32[]{:S(2)}) collective-permute-start(bf16[2,456,128]{2,1,0:T(8,128)(2,1)S(1)} %pad_maximum_fusion.2), channel_id=1, source_target_pairs={{0,1},{1,2},{2,3},{3,0},{4,5},{5,6},{6,7},{7,4},{8,9},{9,10},{10,1... | collective-permute-start | bytes 700424 | tf_op jit(solution)/shard_map/ppermute | solution.py:25
  115.4 0.0 collective-permute-done.8
  115.4 1.9 %collective-permute-start.9 = (bf16[2,456,128]{2,1,0:T(8,128)(2,1)S(1)}, bf16[2,456,128]{2,1,0:T(8,128)(2,1)S(1)}, u32[]{:S(2)}, u32[]{:S(2)}) collective-permute-start(bf16[2,456,128]{2,1,0:T(8,128)(2,1)S(1)} %collective-permute-done.8), channel_id=1, source_target_pairs={{0,1},{1,2},{2,3},{3,0},{4,5},{5,6},{6,7},{7,4},{8,9},{9,10},{10,1... | collective-permute-start | bytes 700424 | tf_op jit(solution)/shard_map/ppermute | solution.py:25
  117.3 0.0 collective-permute-done.5
  117.3 3.9 %collective-permute-start.7 = (bf16[2,456,128]{2,1,0:T(8,128)(2,1)S(1)}, bf16[2,456,128]{2,1,0:T(8,128)(2,1)S(1)}, u32[]{:S(2)}, u32[]{:S(2)}) collective-permute-start(bf16[2,456,128]{2,1,0:T(8,128)(2,1)S(1)} %collective-permute-done.5), channel_id=1, source_target_pairs={{0,3},{1,0},{2,1},{3,2},{4,7},{5,4},{6,5},{7,6},{8,11},{9,8},{10,9... | collective-permute-start | bytes 700424 | tf_op jit(solution)/shard_map/ppermute | solution.py:25
  121.3 0.0 collective-permute-done.6
  121.3 0.0 collective-permute-done.10
  121.3 2.1 %collective-permute-done.9 = bf16[2,456,128]{2,1,0:T(8,128)(2,1)S(1)} collective-permute-done((bf16[2,456,128]{2,1,0:T(8,128)(2,1)S(1)}, bf16[2,456,128]{2,1,0:T(8,128)(2,1)S(1)}, u32[]{:S(2)}, u32[]{:S(2)}) %collective-permute-start.9) | collective-permute-done | bytes 233504 | tf_op jit(solution)/shard_map/ppermute | solution.py:25
  123.4 3.1 %collective-permute-done.7 = bf16[2,456,128]{2,1,0:T(8,128)(2,1)S(1)} collective-permute-done((bf16[2,456,128]{2,1,0:T(8,128)(2,1)S(1)}, bf16[2,456,128]{2,1,0:T(8,128)(2,1)S(1)}, u32[]{:S(2)}, u32[]{:S(2)}) %collective-permute-start.7) | collective-permute-done | bytes 233504 | tf_op jit(solution)/shard_map/ppermute | solution.py:25
  126.5 5.8 %convolve_edges.1 = bf16[25,16,128]{2,1,0:T(8,128)(2,1)} custom-call(s32[2]{0:T(128)S(1)} %pad_add_fusion.refs_0_, bf16[2,57,8,128]{3,2,1,0:T(8,128)(2,1)S(1)} %pad_maximum_fusion.refs_1_, bf16[2,57,8,128]{3,2,1,0:T(8,128)(2,1)S(1)} %pad_maximum_fusion.1.refs_2_, bf16[2,57,8,128]{3,2,1,0:T(8,128)(2,1)S(1)} %bitcast.57, bf16[2,57,8,128]{3,2,1,0:T(8,128)(2,1)S(1)} %bitcast.58, ...), custom_call_target="tpu_custom_call" | custom-call | tf_op jit(solution)/shard_map/convolve_edges/pallas_call | solution.py:324
  (17 shorter events, 0.4 us)
Async XLA Ops:
  0.0 13.7 %copy-start = (bf16[1,13,25,1152]{3,1,2,0:T(8,128)(2,1)S(1)}, bf16[1,13,25,1152]{3,1,2,0:T(8,128)(2,1)}, u32[]{:S(2)}) copy-start(bf16[1,13,25,1152]{3,1,2,0:T(8,128)(2,1)} %param.14) | copy-start | bytes 2246404
  2.3 36.6 %all-to-all-start = ((bf16[8,456,128]{2,1,0:T(8,128)(2,1)}), bf16[8,456,128]{2,1,0:T(8,128)(2,1)S(1)}, u32[]{:S(2)}, u32[]{:S(2)}) async-start(bf16[8,456,128]{2,1,0:T(8,128)(2,1)} %bitcast.65), calls=%async_computation | async-start | bytes 1867776 | tf_op jit(solution)/shard_map/all_to_all | solution.py:367
  15.0 8.4 %copy-start.3 = (f32[1,1152]{1,0:T(1,128)S(1)}, f32[1,1152]{1,0:T(1,128)}, u32[]{:S(2)}) copy-start(f32[1,1152]{1,0:T(1,128)} %param.13) | copy-start | bytes 13828
  15.0 8.4 %copy-start.4 = (s32[1,1152]{1,0:T(1,128)S(1)}, s32[1,1152]{1,0:T(1,128)}, u32[]{:S(2)}) copy-start(s32[1,1152]{1,0:T(1,128)} %param.12) | copy-start | bytes 13828
  23.4 0.7 copy-start.2
  23.5 0.8 copy-start.5
  23.5 18.5 %copy-start.1 = (bf16[1,16,25,128]{3,1,2,0:T(8,128)(2,1)S(1)}, bf16[1,16,25,128]{3,1,2,0:T(8,128)(2,1)}, u32[]{:S(2)}) copy-start(bf16[1,16,25,128]{3,1,2,0:T(8,128)(2,1)} %param.9) | copy-start | bytes 307204
  40.0 12.4 %collective-permute-start = (bf16[2,456,128]{2,1,0:T(8,128)(2,1)S(1)}, bf16[2,456,128]{2,1,0:T(8,128)(2,1)S(1)}, u32[]{:S(2)}, u32[]{:S(2)}) collective-permute-start(bf16[2,456,128]{2,1,0:T(8,128)(2,1)S(1)} %bitcast.63), channel_id=1, source_target_pairs={{0,16},{16,0},{1,17},{17,1},{2,18},{18,2},{3,19},{19,3},{4,20},{20... | collective-permute-start | bytes 700424 | tf_op jit(solution)/shard_map/ppermute | solution.py:25
  42.1 16.4 %collective-permute-start.11 = (bf16[400,128]{1,0:T(8,128)(2,1)S(1)}, bf16[400,128]{1,0:T(8,128)(2,1)S(1)}, u32[]{:S(2)}, u32[]{:S(2)}) collective-permute-start(bf16[400,128]{1,0:T(8,128)(2,1)S(1)} %reshape_squeeze.3), channel_id=1, source_target_pairs={{0,12},{4,0},{8,4},{12,8},{1,13},{5,1},{9,5},{13,9},{2,14},{6,2},{... | collective-permute-start | bytes 307208 | tf_op jit(solution)/shard_map/ppermute | solution.py:25
  47.6 24.8 %collective-permute-start.12 = (bf16[400,128]{1,0:T(8,128)(2,1)S(1)}, bf16[400,128]{1,0:T(8,128)(2,1)S(1)}, u32[]{:S(2)}, u32[]{:S(2)}) collective-permute-start(bf16[400,128]{1,0:T(8,128)(2,1)S(1)} %reshape_squeeze.3), channel_id=1, source_target_pairs={{0,8},{4,12},{8,0},{12,4},{1,9},{5,13},{9,1},{13,5},{2,10},{6,14},... | collective-permute-start | bytes 307208 | tf_op jit(solution)/shard_map/ppermute | solution.py:25
  49.5 22.9 %collective-permute-start.13 = (bf16[400,128]{1,0:T(8,128)(2,1)S(1)}, bf16[400,128]{1,0:T(8,128)(2,1)S(1)}, u32[]{:S(2)}, u32[]{:S(2)}) collective-permute-start(bf16[400,128]{1,0:T(8,128)(2,1)S(1)} %reshape_squeeze.3), channel_id=1, source_target_pairs={{0,4},{4,8},{8,12},{12,0},{1,5},{5,9},{9,13},{13,1},{2,6},{6,10},{... | collective-permute-start | bytes 307208 | tf_op jit(solution)/shard_map/ppermute | solution.py:25
  52.5 10.6 %collective-permute-start.1 = (bf16[456,128]{1,0:T(8,128)(2,1)S(1)}, bf16[456,128]{1,0:T(8,128)(2,1)S(1)}, u32[]{:S(2)}, u32[]{:S(2)}) collective-permute-start(bf16[456,128]{1,0:T(8,128)(2,1)S(1)} %fusion), channel_id=1, source_target_pairs={{0,256},{256,0},{1,257},{257,1},{2,258},{258,2},{3,259},{259,3},{4... | collective-permute-start | bytes 350216 | tf_op jit(solution)/shard_map/ppermute | solution.py:25
  63.2 19.0 %collective-permute-start.3 = (bf16[456,128]{1,0:T(8,128)(2,1)S(1)}, bf16[456,128]{1,0:T(8,128)(2,1)S(1)}, u32[]{:S(2)}, u32[]{:S(2)}) collective-permute-start(bf16[456,128]{1,0:T(8,128)(2,1)S(1)} %add_convert_fusion), channel_id=1, source_target_pairs={{0,8},{4,12},{8,0},{12,4},{1,9},{5,13},{9,1},{13,5},{2,10},{6,14},... | collective-permute-start | bytes 350216 | tf_op jit(solution)/shard_map/ppermute | solution.py:25
  69.7 17.5 %collective-permute-start.4 = (bf16[456,128]{1,0:T(8,128)(2,1)S(1)}, bf16[456,128]{1,0:T(8,128)(2,1)S(1)}, u32[]{:S(2)}, u32[]{:S(2)}) collective-permute-start(bf16[456,128]{1,0:T(8,128)(2,1)S(1)} %add_convert_fusion), channel_id=1, source_target_pairs={{0,4},{4,8},{8,12},{12,0},{1,5},{5,9},{9,13},{13,1},{2,6},{6,10},{... | collective-permute-start | bytes 350216 | tf_op jit(solution)/shard_map/ppermute | solution.py:25
  72.4 23.0 %collective-permute-start.14 = (bf16[1600,128]{1,0:T(8,128)(2,1)S(1)}, bf16[1600,128]{1,0:T(8,128)(2,1)S(1)}, u32[]{:S(2)}, u32[]{:S(2)}) collective-permute-start(bf16[1600,128]{1,0:T(8,128)(2,1)S(1)} %constant_dynamic-update-slice_fusion), channel_id=1, source_target_pairs={{0,3},{1,0},{2,1},{3,2},{4,7},{5,4},{6,5},{7,6},{8,11},{9,8},{10,9... | collective-permute-start | bytes 1228808 | tf_op jit(solution)/shard_map/ppermute | solution.py:25
  75.2 20.2 %collective-permute-start.15 = (bf16[1600,128]{1,0:T(8,128)(2,1)S(1)}, bf16[1600,128]{1,0:T(8,128)(2,1)S(1)}, u32[]{:S(2)}, u32[]{:S(2)}) collective-permute-start(bf16[1600,128]{1,0:T(8,128)(2,1)S(1)} %constant_dynamic-update-slice_fusion), channel_id=1, source_target_pairs={{0,2},{1,3},{2,0},{3,1},{4,6},{5,7},{6,4},{7,5},{8,10},{9,11},{10,... | collective-permute-start | bytes 1228808 | tf_op jit(solution)/shard_map/ppermute | solution.py:25
  78.2 21.3 %collective-permute-start.16 = (bf16[1600,128]{1,0:T(8,128)(2,1)S(1)}, bf16[1600,128]{1,0:T(8,128)(2,1)S(1)}, u32[]{:S(2)}, u32[]{:S(2)}) collective-permute-start(bf16[1600,128]{1,0:T(8,128)(2,1)S(1)} %constant_dynamic-update-slice_fusion), channel_id=1, source_target_pairs={{0,1},{1,2},{2,3},{3,0},{4,5},{5,6},{6,7},{7,4},{8,9},{9,10},{10,1... | collective-permute-start | bytes 1228808 | tf_op jit(solution)/shard_map/ppermute | solution.py:25
  82.2 7.9 %collective-permute-start.2 = (bf16[456,128]{1,0:T(8,128)(2,1)S(1)}, bf16[456,128]{1,0:T(8,128)(2,1)S(1)}, u32[]{:S(2)}, u32[]{:S(2)}) collective-permute-start(bf16[456,128]{1,0:T(8,128)(2,1)S(1)} %add_convert_fusion), channel_id=1, source_target_pairs={{0,12},{4,0},{8,4},{12,8},{1,13},{5,1},{9,5},{13,9},{2,14},{6,2},{... | collective-permute-start | bytes 350216 | tf_op jit(solution)/shard_map/ppermute | solution.py:25
  87.3 28.1 %collective-permute-start.8 = (bf16[2,456,128]{2,1,0:T(8,128)(2,1)S(1)}, bf16[2,456,128]{2,1,0:T(8,128)(2,1)S(1)}, u32[]{:S(2)}, u32[]{:S(2)}) collective-permute-start(bf16[2,456,128]{2,1,0:T(8,128)(2,1)S(1)} %pad_maximum_fusion.3), channel_id=1, source_target_pairs={{0,1},{1,2},{2,3},{3,0},{4,5},{5,6},{6,7},{7,4},{8,9},{9,10},{10,1... | collective-permute-start | bytes 700424 | tf_op jit(solution)/shard_map/ppermute | solution.py:25
  90.1 27.2 %collective-permute-start.5 = (bf16[2,456,128]{2,1,0:T(8,128)(2,1)S(1)}, bf16[2,456,128]{2,1,0:T(8,128)(2,1)S(1)}, u32[]{:S(2)}, u32[]{:S(2)}) collective-permute-start(bf16[2,456,128]{2,1,0:T(8,128)(2,1)S(1)} %pad_maximum_fusion.2), channel_id=1, source_target_pairs={{0,3},{1,0},{2,1},{3,2},{4,7},{5,4},{6,5},{7,6},{8,11},{9,8},{10,9... | collective-permute-start | bytes 700424 | tf_op jit(solution)/shard_map/ppermute | solution.py:25
  108.3 13.0 %collective-permute-start.6 = (bf16[2,456,128]{2,1,0:T(8,128)(2,1)S(1)}, bf16[2,456,128]{2,1,0:T(8,128)(2,1)S(1)}, u32[]{:S(2)}, u32[]{:S(2)}) collective-permute-start(bf16[2,456,128]{2,1,0:T(8,128)(2,1)S(1)} %pad_maximum_fusion.3), channel_id=1, source_target_pairs={{0,3},{1,0},{2,1},{3,2},{4,7},{5,4},{6,5},{7,6},{8,11},{9,8},{10,9... | collective-permute-start | bytes 700424 | tf_op jit(solution)/shard_map/ppermute | solution.py:25
  110.2 11.1 %collective-permute-start.10 = (bf16[2,456,128]{2,1,0:T(8,128)(2,1)S(1)}, bf16[2,456,128]{2,1,0:T(8,128)(2,1)S(1)}, u32[]{:S(2)}, u32[]{:S(2)}) collective-permute-start(bf16[2,456,128]{2,1,0:T(8,128)(2,1)S(1)} %pad_maximum_fusion.2), channel_id=1, source_target_pairs={{0,1},{1,2},{2,3},{3,0},{4,5},{5,6},{6,7},{7,4},{8,9},{9,10},{10,1... | collective-permute-start | bytes 700424 | tf_op jit(solution)/shard_map/ppermute | solution.py:25
  115.4 8.0 %collective-permute-start.9 = (bf16[2,456,128]{2,1,0:T(8,128)(2,1)S(1)}, bf16[2,456,128]{2,1,0:T(8,128)(2,1)S(1)}, u32[]{:S(2)}, u32[]{:S(2)}) collective-permute-start(bf16[2,456,128]{2,1,0:T(8,128)(2,1)S(1)} %collective-permute-done.8), channel_id=1, source_target_pairs={{0,1},{1,2},{2,3},{3,0},{4,5},{5,6},{6,7},{7,4},{8,9},{9,10},{10,1... | collective-permute-start | bytes 700424 | tf_op jit(solution)/shard_map/ppermute | solution.py:25
  117.3 9.2 %collective-permute-start.7 = (bf16[2,456,128]{2,1,0:T(8,128)(2,1)S(1)}, bf16[2,456,128]{2,1,0:T(8,128)(2,1)S(1)}, u32[]{:S(2)}, u32[]{:S(2)}) collective-permute-start(bf16[2,456,128]{2,1,0:T(8,128)(2,1)S(1)} %collective-permute-done.5), channel_id=1, source_target_pairs={{0,3},{1,0},{2,1},{3,2},{4,7},{5,4},{6,5},{7,6},{8,11},{9,8},{10,9... | collective-permute-start | bytes 700424 | tf_op jit(solution)/shard_map/ppermute | solution.py:25
